TPU v7x, 32 devices: a whole 2x2x4 slice. The times are simulated.
32 devices in a mesh: groups: 1, ctx: 32 (over z, y, x, core), kv: 1.
Axes of the slice: x: 2, y: 2, z: 4, core: 2. Of those that a mesh axis runs over, the one named last changes fastest.
Arguments:
- queries: bfloat16 [128, 64, 128], P('groups', 'kv'), may hold values from -10 to 10
- cache_keys: bfloat16 [32768, 4, 128], P(('groups', 'ctx'), 'kv'), may hold values from -5 to 5
- cache_values: bfloat16 [32768, 4, 128], P(('groups', 'ctx'), 'kv'), may hold values from -5 to 5
- block_mask: int32 [1, 256], P('groups', 'ctx'), may hold values from 0 to 1
- key_counts: int32 [256], P(('groups', 'ctx')), may hold values from 1 to 128, as said below
- out_weight: bfloat16 [8192, 16384], P('kv', 'ctx'), may hold values from -0.25 to 0.25
Outputs:
- layer_out: float32 [128, 16384], P(('groups', 'kv'), 'ctx')
Inputs may be any that keep to these rules, and one draw needn't show every extreme that they name: `key_counts`: key block 0 is full.
All inputs are finite; a program needn't handle non-finite values.
Results may differ from a plain program's by a relative error of at most 0.0065.
Values may be sent and summed in bfloat16 or wider, within the bound.
No kernel may reach another device: no remote copies, remote signals or barrier semaphores. Data moves between devices by JAX's collectives and lax.ppermute only.
A program may use at most 64 MiB of HBM per device.

v0:
```python
import functools
import math

import jax
import jax.numpy as jnp
from jax import lax
from jax.experimental import pallas as pl
from jax.experimental.pallas import tpu as pltpu
from jax.sharding import PartitionSpec as P

BLK = 128
LANES = 128
STAT = 8
very_low = -1e30
lowest_top = -(2.0**99)
bf16 = jnp.bfloat16
f32 = jnp.float32


def pack_state(out, top, total):
    high = total.astype(bf16).astype(f32)
    low = total - high
    row = lax.broadcasted_iota(jnp.int32, (STAT, LANES), 0)
    stats = jnp.where(row == 0, top, jnp.where(row == 1, high, jnp.where(row == 2, low, 0.0)))
    return out.astype(bf16), stats.astype(bf16)


def active_count(meta):
    block_count = (meta.shape[0] - 2) // 2
    return sum((meta[2 + block] > 0).astype(jnp.int32) for block in range(block_count))


def split_kernel(meta, k_hbm, v_hbm, q_hbm, kd, vt, sent_ref, *scratch):
    listed, kept_counts, q_ref, k_ref, v_ref, spread, sems = scratch
    d = k_hbm.shape[1]
    kv_count = kd.shape[0]
    group_size = q_ref.shape[1]
    block_count = (meta.shape[0] - 2) // 2
    group = 1 - meta[0]

    heads = pl.ds(pl.multiple_of(group * group_size, group_size), group_size)
    copies = [
        pltpu.make_async_copy(k_hbm, k_ref, sems.at[0]),
        pltpu.make_async_copy(v_hbm, v_ref, sems.at[1]),
        pltpu.make_async_copy(q_hbm.at[:, heads, :], q_ref, sems.at[2]),
    ]
    for copy in copies:
        copy.start()

    def note(block, found):
        listed[found] = block
        kept_counts[found] = meta[2 + block_count + block]
        return found + (meta[2 + block] > 0).astype(jnp.int32)

    active = lax.fori_loop(0, block_count, note, jnp.int32(0))
    place = lax.broadcasted_iota(jnp.int32, (BLK, LANES), 0)
    across = lax.broadcasted_iota(jnp.int32, (STAT, LANES), 1)

    def split(source, position):
        start = pl.multiple_of(listed[position] * (BLK * kv_count), BLK * kv_count)
        spread[...] = source[pl.ds(start, BLK * kv_count), :].astype(f32)
        return [spread[pl.ds(g, BLK, stride=kv_count), :] for g in range(kv_count)]

    def fetch_keys(position, carry):
        at = pl.ds(pl.multiple_of(position * BLK, BLK), BLK)
        valid = place < kept_counts[position]
        for g, key in enumerate(split(k_ref, position)):
            kd[g, at, :] = jnp.where(valid, key, key[0:1]).astype(bf16)
        return carry

    def fetch_values(position, carry):
        at = pl.ds(pl.multiple_of(position * BLK, BLK), BLK)
        count = kept_counts[position]
        for g, value in enumerate(split(v_ref, position)):
            vt[g, 0:d, at] = jnp.where(place < count, value, 0.0).T.astype(bf16)
            vt[g, d:, at] = (across < count).astype(f32).astype(bf16)
        return carry

    copies[0].wait()
    lax.fori_loop(0, active, fetch_keys, 0)
    copies[1].wait()
    lax.fori_loop(0, active, fetch_values, 0)

    @pl.when(active % 2 == 1)
    def _():
        at = pl.ds(pl.multiple_of(active * BLK, BLK), BLK)
        before = pl.ds(pl.multiple_of((active - 1) * BLK, BLK), BLK)
        for g in range(kv_count):
            kd[g, at, :] = kd[g, before, :]
            vt[g, :, at] = jnp.zeros((d + STAT, BLK), bf16)

    copies[2].wait()
    attend_all(active, [(sent_ref, group, lambda: q_ref[...])], kd, vt)


def attention_kernel(chunk_roles, meta, kd, vt, q_ref, *outs):
    group_size = q_ref.shape[1] // kd.shape[0]
    todo = []
    for out, (chunk, is_other) in zip(outs, chunk_roles):
        group = 2 * chunk + (1 - meta[0] if is_other else meta[0])

        def read(group=group):
            heads = pl.ds(pl.multiple_of(group * group_size, group_size), group_size)
            return q_ref[:, heads, :]

        todo.append((out, group, read))
    attend_all(active_count(meta), todo, kd, vt)


def attend_all(active, todo, kd, vt):
    d = kd.shape[2]
    scale2 = math.log2(math.e) / math.sqrt(d)
    rows = todo[0][0].shape[0] * LANES
    pairs = (active + 1) // 2

    def attend(width, out, group, read):
        q = read().reshape(rows, d)
        scores = lax.dot_general(
            kd[group, 0:width, :], q, (((1,), (1,)), ((), ())), preferred_element_type=f32
        )
        top = (jnp.max(scores, axis=0, keepdims=True) * scale2).astype(bf16).astype(f32)
        weights = jnp.exp2(scores * scale2 - top).astype(bf16)
        sums = jnp.dot(vt[group, :, 0:width], weights, preferred_element_type=f32)
        total = sums[d:]
        high = total.astype(bf16).astype(f32)
        row = lax.broadcasted_iota(jnp.int32, (STAT, rows), 0)
        stats = jnp.where(row == 0, top, jnp.where(row == 1, high, total - high)).astype(bf16)
        value = sums[:d].astype(bf16)
        for piece in range(rows // LANES):
            at = slice(piece * LANES, (piece + 1) * LANES)
            out[piece, 0:d] = value[:, at]
            out[piece, d:] = stats[:, at]

    for n in range(1, kd.shape[1] // (2 * BLK) + 1):

        @pl.when(pairs == n)
        def _(n=n):
            for out, group, read in todo:
                attend(2 * BLK * n, out, group, read)

    @pl.when(pairs == 0)
    def _():
        row = lax.broadcasted_iota(jnp.int32, (d + STAT, LANES), 0)
        empty = jnp.where(row == d, lowest_top, 0.0).astype(bf16)
        for out, _, _ in todo:
            for piece in range(rows // LANES):
                out[piece] = empty


def merged(parts, d):
    stats = [part[d : d + STAT, :].astype(f32) for part in parts]
    tops = [stat[0:1] for stat in stats]
    top = functools.reduce(jnp.maximum, tops)
    out, total = 0.0, 0.0
    for part, stat, one in zip(parts, stats, tops):
        factor = jnp.exp2(one - top)
        out = out + part[0:d, :].astype(f32) * factor
        total = total + (stat[1:2] + stat[2:3]) * factor
    return out, top, total


def store_merged(ref, z, parts):
    d = ref.shape[1] - STAT
    out, stats = pack_state(*merged(parts, d))
    ref[z, 0:d, :] = out
    ref[z, d : d + STAT, :] = stats


def plane_chips(meta):
    core, my_xy = meta[0], meta[1]
    return [my_xy, my_xy ^ (1 + core), my_xy ^ (2 - core), my_xy ^ 3]


def core_kernel(meta, kept, received, *outs):
    z_size = outs[0].shape[0]
    for chip, out in zip(plane_chips(meta), outs):
        for z in range(z_size):
            piece = chip * z_size + z
            store_merged(out, z, [kept[piece], received[piece]])


def plane_kernel(*refs):
    ins, out = refs[:-1], refs[-1]
    for z in range(out.shape[0]):
        store_merged(out, z, [ref[z] for ref in ins])


def last_kernel(*refs):
    ins, out_ref, turned = refs[:-2], refs[-2], refs[-1]
    d = ins[0].shape[1] - STAT
    tokens = out_ref.shape[1]
    heads = LANES // tokens
    for z in range(out_ref.shape[0]):
        out, _, total = merged([ref[z] for ref in ins], d)
        turned[z] = (out / total).T
        for h in range(heads):
            picked = turned[z, pl.ds(h, tokens, stride=heads), :]
            out_ref[z, :, h * d : (h + 1) * d] = picked.astype(bf16)


def project_kernel(terms, has_earlier, last, meta, weight, *refs):
    z_size, tokens, depth = refs[0].shape
    total = refs[4 * len(terms)][...] if has_earlier else None
    out_ref = refs[-1]
    for i, (chunk, is_other) in enumerate(terms):
        left = jnp.concatenate(
            [part[...].reshape(z_size * tokens, depth) for part in refs[4 * i : 4 * i + 4]], axis=0
        )
        group = 2 * chunk + (1 - meta[0] if is_other else meta[0])
        at = pl.ds(pl.multiple_of(group * depth, depth), depth)
        product = jnp.dot(left, weight[at, :], preferred_element_type=f32)
        total = product if total is None else total + product
    if not last:
        out_ref[...] = total
        return
    size = z_size * tokens
    for j, chip in enumerate(plane_chips(meta)):
        to = pl.ds(pl.multiple_of(chip * size, size), size)
        out_ref[to, :] = total[j * size : (j + 1) * size]


def hop(value, mask):
    pairs = [(source, source ^ mask) for source in range(lax.axis_size("ctx"))]
    return lax.ppermute(value, "ctx", pairs)


def plane_hop(value, number):
    masks = {1: (2, 4), 2: (4, 2), 3: (6, 6)}[number]
    pairs = [(source, source ^ masks[source % 2]) for source in range(lax.axis_size("ctx"))]
    return lax.ppermute(value, "ctx", pairs)


def line_hop(value, reach, z_size):
    masks = (8 * reach, 4 * z_size // reach)
    pairs = [(source, source ^ masks[source % 2]) for source in range(lax.axis_size("ctx"))]
    return lax.ppermute(value, "ctx", pairs)


VMEM = pl.BlockSpec(memory_space=pltpu.VMEM)
SMEM = pl.BlockSpec(memory_space=pltpu.SMEM)
HBM = pl.BlockSpec(memory_space=pltpu.HBM)
SMALL = pltpu.CompilerParams(vmem_limit_bytes=4 << 20)


def fast_body(queries, cache_keys, cache_values, block_mask, key_counts, out_weight):
    index = lax.axis_index("ctx")
    z_size = lax.axis_size("ctx") // 8
    token_count, head_count, d = queries.shape
    kv_count = cache_keys.shape[1]
    group_size = head_count // kv_count
    rows = token_count * group_size
    pieces = rows // LANES
    positions = cache_keys.shape[0]
    features = out_weight.shape[1]
    core = index & 1
    my_xy = (index >> 1) & 3
    tall = d + STAT
    keys = cache_keys.reshape(positions * kv_count, d)
    values = cache_values.reshape(positions * kv_count, d)
    place = jnp.concatenate(
        [jnp.stack([core, my_xy]).astype(jnp.int32), block_mask[0], key_counts]
    )
    kept_in_hbm = functools.partial(pltpu.with_memory_space_constraint, memory_space=pltpu.HBM)
    state = jax.ShapeDtypeStruct((z_size, tall, LANES), bf16)

    partial = jax.ShapeDtypeStruct((pieces, tall, LANES), bf16)
    blocks = positions // BLK

    def split_and_attend():
        return pl.pallas_call(
            split_kernel,
            in_specs=[SMEM] + [HBM] * 3,
            out_specs=[VMEM] * 3,
            scratch_shapes=[
                pltpu.SMEM((blocks + 1,), jnp.int32),
                pltpu.SMEM((blocks + 1,), jnp.int32),
                pltpu.VMEM((token_count, group_size, d), bf16),
                pltpu.VMEM((positions * kv_count, d), bf16),
                pltpu.VMEM((positions * kv_count, d), bf16),
                pltpu.VMEM((BLK * kv_count, d), f32),
                pltpu.SemaphoreType.DMA((3,)),
            ],
            out_shape=[
                jax.ShapeDtypeStruct((kv_count, positions, d), bf16),
                jax.ShapeDtypeStruct((kv_count, tall, positions), bf16),
                partial,
            ],
            compiler_params=pltpu.CompilerParams(vmem_limit_bytes=32 << 20),
            cost_estimate=pl.CostEstimate(
                flops=4 * rows * positions * d,
                transcendentals=rows * positions,
                bytes_accessed=4 * positions * d * kv_count,
            ),
            name="split_and_attend",
        )(place, kept_in_hbm(keys), kept_in_hbm(values), kept_in_hbm(queries))

    def attend(chunk_roles, kd, vt):
        count = len(chunk_roles)
        return pl.pallas_call(
            functools.partial(attention_kernel, chunk_roles),
            in_specs=[SMEM] + [VMEM] * 3,
            out_specs=[VMEM] * count,
            out_shape=[partial] * count,
            compiler_params=pltpu.CompilerParams(vmem_limit_bytes=32 << 20),
            cost_estimate=pl.CostEstimate(
                flops=4 * count * rows * positions * d,
                transcendentals=count * rows * positions,
                bytes_accessed=4 * positions * d * count,
            ),
            name="attend",
        )(place, kd, vt, queries)

    def merge_cores(kept, received):
        return pl.pallas_call(
            core_kernel,
            in_specs=[SMEM] + [VMEM] * 2,
            out_specs=[VMEM] * 4,
            out_shape=[state] * 4,
            compiler_params=SMALL,
            name="merge_cores",
        )(place, kept, received)

    def merge_chips(parts):
        return pl.pallas_call(
            plane_kernel,
            in_specs=[VMEM] * len(parts),
            out_specs=VMEM,
            out_shape=state,
            compiler_params=SMALL,
            name="merge_chips",
        )(*parts)

    def finish(parts):
        tokens = LANES // group_size
        return pl.pallas_call(
            last_kernel,
            in_specs=[VMEM] * len(parts),
            out_specs=VMEM,
            out_shape=jax.ShapeDtypeStruct((z_size, tokens, group_size * d), bf16),
            scratch_shapes=[pltpu.VMEM((z_size, LANES, d), f32)],
            compiler_params=SMALL,
            name="finish",
        )(*parts)

    def project(terms, parts, earlier, last=False):
        depth = group_size * d
        more = [] if earlier is None else [earlier]
        return pl.pallas_call(
            functools.partial(project_kernel, terms, bool(more), last),
            in_specs=[SMEM] + [VMEM] * (1 + len(parts) + len(more)),
            out_specs=VMEM,
            out_shape=jax.ShapeDtypeStruct((token_count, features), f32),
            compiler_params=pltpu.CompilerParams(vmem_limit_bytes=8 << 20),
            cost_estimate=pl.CostEstimate(
                flops=2 * len(terms) * token_count * depth * features,
                transcendentals=0,
                bytes_accessed=2 * len(terms) * depth * features,
            ),
            name="project",
        )(place, out_weight, *parts, *more)

    def exchange_plane(parts):
        return [parts[0]] + [plane_hop(parts[j], j) for j in (1, 2, 3)]

    def exchange_line(parts):
        part = merge_chips(parts)
        reach = 1
        while 2 * reach < z_size:
            part = merge_chips([part, line_hop(part, reach, z_size)])
            reach *= 2
        return finish([part, line_hop(part, reach, z_size)])

    def gather_plane(attended):
        first, second = plane_hop(attended, 1), plane_hop(attended, 2)
        return [attended, first, second, plane_hop(first, 2)]

    kd, vt, sent = split_and_attend()
    received = hop(sent, 1)
    kept, sent = attend([(0, False), (1, True)], kd, vt)
    next_received = hop(sent, 1)
    parts = merge_cores(kept, received)
    parts, kd = lax.optimization_barrier((parts, kd))
    first = exchange_plane(parts)
    (kept,) = attend([(1, False)], kd, vt)
    parts = merge_cores(kept, next_received)
    parts, first[0] = lax.optimization_barrier((parts, first[0]))
    second = exchange_plane(parts)
    own = gather_plane(exchange_line(first))
    other = [hop(own[j], 1) for j in (0, 2, 1, 3)]
    next_own = gather_plane(exchange_line(second))
    next_other = [hop(next_own[j], 1) for j in (0, 2, 1, 3)]
    total = project([(0, False), (0, True), (1, False)], own + other + next_own, None)
    return project([(1, True)], next_other, total, last=True)


def partner_of(value, axis, distance):
    mask = 2**distance
    pairs = [(source, source ^ mask) for source in range(lax.axis_size(axis))]
    return lax.ppermute(value, axis, pairs)


def combine(earlier, later):
    out_one, top_one, sum_one = earlier
    out_two, top_two, sum_two = later
    new_top = jnp.maximum(top_one, top_two)
    factor_one = jnp.exp(top_one - new_top)
    factor_two = jnp.exp(top_two - new_top)
    new_out = out_one * factor_one[..., None] + out_two * factor_two[..., None]
    return (new_out, new_top, sum_one * factor_one + sum_two * factor_two)


def keep_state(key_block, run_state):
    return run_state


def partial_rows(rows_q, row_mask, cache_keys, cache_values, key_counts):
    row_count, head_count, head_size = rows_q.shape
    kv_count = cache_keys.shape[1]
    group_size = head_count // kv_count
    grouped = rows_q.reshape(row_count, kv_count, group_size, head_size)
    block_count = cache_keys.shape[0] // BLK
    score_scale = 1.0 / math.sqrt(head_size)
    offsets = jnp.arange(BLK, dtype=jnp.int32)

    def update(key_block, run_state):
        out_sum, top_score, weight_sum = run_state
        key_part = lax.dynamic_slice_in_dim(cache_keys, key_block * BLK, BLK, 0)
        value_part = lax.dynamic_slice_in_dim(cache_values, key_block * BLK, BLK, 0)
        scores = (
            jnp.einsum("rgqd,kgd->rgqk", grouped, key_part, preferred_element_type=jnp.float32)
            * score_scale
        )
        active_rows = lax.dynamic_slice_in_dim(row_mask, key_block, 1, 1)[:, 0] > 0
        valid_count = lax.dynamic_slice_in_dim(key_counts, key_block, 1, 0)[0]
        valid = active_rows[:, None, None, None] & (offsets < valid_count)[None, None, None, :]
        scores = jnp.where(valid, scores, very_low)
        new_top = jnp.maximum(top_score, jnp.max(scores, axis=-1))
        weights = jnp.where(valid, jnp.exp(scores - new_top[..., None]), 0.0)
        factor = jnp.exp(top_score - new_top)
        new_sum = weight_sum * factor + jnp.sum(weights, axis=-1)
        new_out = out_sum * factor[..., None] + jnp.einsum(
            "rgqk,kgd->rgqd",
            weights.astype(jnp.bfloat16),
            value_part,
            preferred_element_type=jnp.float32,
        )
        return (new_out, new_top, new_sum)

    def visit_block(key_block, run_state):
        active = jnp.any(lax.dynamic_slice_in_dim(row_mask, key_block, 1, 1) > 0)
        return lax.cond(active, update, keep_state, key_block, run_state)

    initial = (
        jnp.zeros((row_count, kv_count, group_size, head_size), jnp.float32),
        jnp.full((row_count, kv_count, group_size), very_low, jnp.float32),
        jnp.zeros((row_count, kv_count, group_size), jnp.float32),
    )
    return lax.fori_loop(0, block_count, visit_block, initial)


def general_body(queries, cache_keys, cache_values, block_mask, key_counts, out_weight):
    cycle_size = lax.axis_size("ctx")
    cycle_index = lax.axis_index("ctx")
    token_count, head_count, head_size = queries.shape
    segment = token_count // cycle_size
    query_blocks = queries.reshape(block_mask.shape[0], BLK, head_count, head_size)

    def per_block(block_item):
        rows_q, mask_row = block_item
        row_mask = jnp.broadcast_to(mask_row[None, :], (BLK, mask_row.shape[0]))
        return partial_rows(rows_q, row_mask, cache_keys, cache_values, key_counts)

    stacked = lax.map(per_block, (query_blocks, block_mask))
    run_state = tuple((part.reshape((token_count,) + part.shape[2:]) for part in stacked))
    bit_total = cycle_size.bit_length() - 1
    for bit_number in range(bit_total - 1, -1, -1):
        half_rows = run_state[1].shape[0] // 2
        upper_half = jnp.bitwise_and(jnp.right_shift(cycle_index, bit_number), 1)
        kept = tuple(
            (
                lax.dynamic_slice_in_dim(part, upper_half * half_rows, half_rows, 0)
                for part in run_state
            )
        )
        outgoing = tuple(
            (
                lax.dynamic_slice_in_dim(part, (1 - upper_half) * half_rows, half_rows, 0)
                for part in run_state
            )
        )
        received = partner_of((outgoing[0], outgoing[1], outgoing[2]), "ctx", bit_number)
        run_state = combine(kept, received)
    out_sum, top_score, weight_sum = run_state
    attended = (
        (out_sum / weight_sum[..., None])
        .astype(jnp.bfloat16)
        .reshape(segment, head_count * head_size)
    )
    partial_value = jnp.dot(
        lax.all_gather(attended, "ctx", axis=0, tiled=True),
        out_weight,
        preferred_element_type=jnp.float32,
    )
    return lax.psum_scatter(partial_value, "kv", scatter_dimension=0, tiled=True)


def body(queries, cache_keys, cache_values, block_mask, key_counts, out_weight):
    devices = lax.axis_size("ctx")
    token_count, head_count, d = queries.shape
    kv_count = cache_keys.shape[1]
    group_size = head_count // kv_count
    suits = (
        lax.axis_size("kv") == 1
        and devices == 32
        and token_count == BLK
        and block_mask.shape[0] == 1
        and kv_count == 4
        and d == LANES
        and group_size == 16
        and token_count * group_size == LANES * (devices // 2)
    )
    run = fast_body if suits else general_body
    return run(queries, cache_keys, cache_values, block_mask, key_counts, out_weight)


def solution(mesh):
    placed = (
        P("groups", "kv", None),
        P(("groups", "ctx"), "kv", None),
        P(("groups", "ctx"), "kv", None),
        P("groups", "ctx"),
        P(("groups", "ctx")),
        P("kv", "ctx"),
    )
    return jax.shard_map(
        body, mesh=mesh, in_specs=placed, out_specs=P(("groups", "kv"), "ctx"), check_vma=False
    )
```

profile of v0, /device:TPU:0, one launch (start us, length us, event | category | flops | bytes accessed | tf_op | source)
XLA Modules:
  0.0 59.5 jit_solution(14392514432196358887)
XLA Ops:
  0.0 0.7 %pad_add_fusion.meta = s32[18]{0:T(128)S(1)} fusion(s32[8]{0:T(128)} %param.10, s32[8]{0:T(128)} %bitcast.9, s32[1]{0:T(128)} %bitcast.1, s32[1]{0:T(128)} %bitcast), kind=kLoop, calls=%fused_computation | loop fusion | flops 54 | bytes 144 | tf_op jit(solution)/shard_map/concatenate | solution.py:260
  0.8 3.3 %split_and_attend.1 = (bf16[4,1024,128]{2,1,0:T(8,128)(2,1)S(1)}, bf16[4,136,1024]{2,1,0:T(8,128)(2,1)S(1)}, bf16[16,136,128]{2,1,0:T(8,128)(2,1)S(1)}) custom-call(s32[18]{0:T(128)S(1)} %pad_add_fusion.meta, bf16[4096,128]{1,0:T(8,128)(2,1)} %bitcast.7, bf16[4096,128]{1,0:T(8,128)(2,1)} %bitcast.8, bf16[128,64,128]{2,1,0:T(8,128)(2,1)} %q_ref.3), custom_call_target="tpu_custom_call" | custom-call | flops 1073741824 | bytes 2097152 | tf_op jit(solution)/shard_map/split_and_attend/pallas_call | solution.py:270
  4.0 1.4 %collective-permute-start = (bf16[16,136,128]{2,1,0:T(8,128)(2,1)S(1)}, bf16[16,136,128]{2,1,0:T(8,128)(2,1)S(1)}, u32[]{:S(2)}, u32[]{:S(2)}) collective-permute-start(bf16[16,136,128]{2,1,0:T(8,128)(2,1)S(1)} %get-tuple-element.31), channel_id=1, source_target_pairs={{0,1},{1,0},{2,3},{3,2},{4,5},{5,4},{6,7},{7,6},{8,9},{9,8},{10,11... | collective-permute-start | bytes 1671176 | tf_op jit(solution)/shard_map/ppermute | solution.py:224
  5.4 2.3 %attend.2 = (bf16[16,136,128]{2,1,0:T(8,128)(2,1)S(1)}, bf16[16,136,128]{2,1,0:T(8,128)(2,1)S(1)}) custom-call(s32[18]{0:T(128)S(1)} %pad_add_fusion.meta, bf16[4,1024,128]{2,1,0:T(8,128)(2,1)S(1)} %get-tuple-element.36.kd, bf16[4,136,1024]{2,1,0:T(8,128)(2,1)S(1)} %get-tuple-element.29.vt, bf16[128,64,128]{2,1,0:T(8,128)(2,1)S(1)} %copy-done), custom_call_target="tpu_custom_call" | custom-call | flops 2147483648 | bytes 1048576 | tf_op jit(solution)/shard_map/attend/pallas_call | solution.py:299
  7.8 1.4 %collective-permute-start.1 = (bf16[16,136,128]{2,1,0:T(8,128)(2,1)S(1)}, bf16[16,136,128]{2,1,0:T(8,128)(2,1)S(1)}, u32[]{:S(2)}, u32[]{:S(2)}) collective-permute-start(bf16[16,136,128]{2,1,0:T(8,128)(2,1)S(1)} %get-tuple-element.37), channel_id=1, source_target_pairs={{0,1},{1,0},{2,3},{3,2},{4,5},{5,4},{6,7},{7,6},{8,9},{9,8},{10,11... | collective-permute-start | bytes 1671176 | tf_op jit(solution)/shard_map/ppermute | solution.py:224
  9.1 0.8 %merge_cores.2 = (bf16[4,136,128]{2,1,0:T(8,128)(2,1)S(1)}, bf16[4,136,128]{2,1,0:T(8,128)(2,1)S(1)}, bf16[4,136,128]{2,1,0:T(8,128)(2,1)S(1)}, bf16[4,136,128]{2,1,0:T(8,128)(2,1)S(1)}) custom-call(s32[18]{0:T(128)S(1)} %pad_add_fusion.meta, bf16[16,136,128]{2,1,0:T(8,128)(2,1)S(1)} %get-tuple-element.30.kept, ...), custom_call_target="tpu_custom_call" | custom-call | tf_op jit(solution)/shard_map/merge_cores/pallas_call | solution.py:314
  10.0 4.6 %collective-permute-start.14 = (bf16[4,136,128]{2,1,0:T(8,128)(2,1)S(1)}, bf16[4,136,128]{2,1,0:T(8,128)(2,1)S(1)}, u32[]{:S(2)}, u32[]{:S(2)}) collective-permute-start(bf16[4,136,128]{2,1,0:T(8,128)(2,1)S(1)} %get-tuple-element.48), channel_id=1, source_target_pairs={{0,2},{1,5},{2,0},{3,7},{4,6},{5,1},{6,4},{7,3},{8,10},{9,13},{10,... | collective-permute-start | bytes 417800 | tf_op jit(solution)/shard_map/ppermute | solution.py:230
  14.6 1.5 %collective-permute-start.15 = (bf16[4,136,128]{2,1,0:T(8,128)(2,1)S(1)}, bf16[4,136,128]{2,1,0:T(8,128)(2,1)S(1)}, u32[]{:S(2)}, u32[]{:S(2)}) collective-permute-start(bf16[4,136,128]{2,1,0:T(8,128)(2,1)S(1)} %get-tuple-element.49), channel_id=1, source_target_pairs={{0,4},{1,3},{2,6},{3,1},{4,0},{5,7},{6,2},{7,5},{8,12},{9,11},{10,... | collective-permute-start | bytes 417800 | tf_op jit(solution)/shard_map/ppermute | solution.py:230
  16.2 1.7 %attend.3.kept = bf16[16,136,128]{2,1,0:T(8,128)(2,1)S(1)} custom-call(s32[18]{0:T(128)S(1)} %pad_add_fusion.meta, bf16[4,1024,128]{2,1,0:T(8,128)(2,1)S(1)} %get-tuple-element.36.kd, bf16[4,136,1024]{2,1,0:T(8,128)(2,1)S(1)} %get-tuple-element.29.vt, bf16[128,64,128]{2,1,0:T(8,128)(2,1)S(1)} %copy-done), custom_call_target="tpu_custom_call" | custom-call | flops 1073741824 | bytes 524288 | tf_op jit(solution)/shard_map/attend/pallas_call | solution.py:299
  17.8 0.8 %merge_cores.3 = (bf16[4,136,128]{2,1,0:T(8,128)(2,1)S(1)}, bf16[4,136,128]{2,1,0:T(8,128)(2,1)S(1)}, bf16[4,136,128]{2,1,0:T(8,128)(2,1)S(1)}, bf16[4,136,128]{2,1,0:T(8,128)(2,1)S(1)}) custom-call(s32[18]{0:T(128)S(1)} %pad_add_fusion.meta, bf16[16,136,128]{2,1,0:T(8,128)(2,1)S(1)} %attend.3.kept, bf16[16,136,128]{2,1,0:T(8,128)(2,1)S(1)} %collective-permute-done.1.received), custom_call_target="tpu_custom_call" | custom-call | tf_op jit(solution)/shard_map/merge_cores/pallas_call | solution.py:314
  18.7 3.3 %collective-permute-start.2 = (bf16[4,136,128]{2,1,0:T(8,128)(2,1)S(1)}, bf16[4,136,128]{2,1,0:T(8,128)(2,1)S(1)}, u32[]{:S(2)}, u32[]{:S(2)}) collective-permute-start(bf16[4,136,128]{2,1,0:T(8,128)(2,1)S(1)} %get-tuple-element.44), channel_id=1, source_target_pairs={{0,2},{1,5},{2,0},{3,7},{4,6},{5,1},{6,4},{7,3},{8,10},{9,13},{10,... | collective-permute-start | bytes 417800 | tf_op jit(solution)/shard_map/ppermute | solution.py:230
  22.0 1.5 %collective-permute-start.3 = (bf16[4,136,128]{2,1,0:T(8,128)(2,1)S(1)}, bf16[4,136,128]{2,1,0:T(8,128)(2,1)S(1)}, u32[]{:S(2)}, u32[]{:S(2)}) collective-permute-start(bf16[4,136,128]{2,1,0:T(8,128)(2,1)S(1)} %get-tuple-element.45), channel_id=1, source_target_pairs={{0,4},{1,3},{2,6},{3,1},{4,0},{5,7},{6,2},{7,5},{8,12},{9,11},{10,... | collective-permute-start | bytes 417800 | tf_op jit(solution)/shard_map/ppermute | solution.py:230
  23.7 0.6 %collective-permute-start.17 = (bf16[4,136,128]{2,1,0:T(8,128)(2,1)S(1)}, bf16[4,136,128]{2,1,0:T(8,128)(2,1)S(1)}, u32[]{:S(2)}, u32[]{:S(2)}) collective-permute-start(bf16[4,136,128]{2,1,0:T(8,128)(2,1)S(1)} %merge_chips.6.refs_0_), channel_id=1, source_target_pairs={{0,8},{1,17},{2,10},{3,19},{4,12},{5,21},{6,14},{7,23},{8,0},{9,25... | collective-permute-start | bytes 417800 | tf_op jit(solution)/shard_map/ppermute | solution.py:236
  24.3 2.1 %collective-permute-done.2.refs_1_ = bf16[4,136,128]{2,1,0:T(8,128)(2,1)S(1)} collective-permute-done((bf16[4,136,128]{2,1,0:T(8,128)(2,1)S(1)}, bf16[4,136,128]{2,1,0:T(8,128)(2,1)S(1)}, u32[]{:S(2)}, u32[]{:S(2)}) %collective-permute-start.2) | collective-permute-done | bytes 139296 | tf_op jit(solution)/shard_map/ppermute | solution.py:230
  26.4 3.2 %collective-permute-done.3.refs_2_ = bf16[4,136,128]{2,1,0:T(8,128)(2,1)S(1)} collective-permute-done((bf16[4,136,128]{2,1,0:T(8,128)(2,1)S(1)}, bf16[4,136,128]{2,1,0:T(8,128)(2,1)S(1)}, u32[]{:S(2)}, u32[]{:S(2)}) %collective-permute-start.3) | collective-permute-done | bytes 139296 | tf_op jit(solution)/shard_map/ppermute | solution.py:230
  30.0 3.7 %collective-permute-start.18 = (bf16[4,136,128]{2,1,0:T(8,128)(2,1)S(1)}, bf16[4,136,128]{2,1,0:T(8,128)(2,1)S(1)}, u32[]{:S(2)}, u32[]{:S(2)}) collective-permute-start(bf16[4,136,128]{2,1,0:T(8,128)(2,1)S(1)} %merge_chips.7.refs_0_), channel_id=1, source_target_pairs={{0,16},{1,9},{2,18},{3,11},{4,20},{5,13},{6,22},{7,15},{8,24},{9,1... | collective-permute-start | bytes 417800 | tf_op jit(solution)/shard_map/ppermute | solution.py:236
  33.7 3.7 %collective-permute-done.5.refs_1_ = bf16[4,136,128]{2,1,0:T(8,128)(2,1)S(1)} collective-permute-done((bf16[4,136,128]{2,1,0:T(8,128)(2,1)S(1)}, bf16[4,136,128]{2,1,0:T(8,128)(2,1)S(1)}, u32[]{:S(2)}, u32[]{:S(2)}) %collective-permute-start.5) | collective-permute-done | bytes 139296 | tf_op jit(solution)/shard_map/ppermute | solution.py:236
  37.5 2.1 %collective-permute-start.6 = (bf16[4,136,128]{2,1,0:T(8,128)(2,1)S(1)}, bf16[4,136,128]{2,1,0:T(8,128)(2,1)S(1)}, u32[]{:S(2)}, u32[]{:S(2)}) collective-permute-start(bf16[4,136,128]{2,1,0:T(8,128)(2,1)S(1)} %merge_chips.5.refs_0_), channel_id=1, source_target_pairs={{0,16},{1,9},{2,18},{3,11},{4,20},{5,13},{6,22},{7,15},{8,24},{9,1... | collective-permute-start | bytes 417800 | tf_op jit(solution)/shard_map/ppermute | solution.py:236
  39.5 0.2 finish.3.refs_0_
  39.8 2.3 %collective-permute-start.19 = (bf16[4,8,2048]{2,1,0:T(8,128)(2,1)S(1)}, bf16[4,8,2048]{2,1,0:T(8,128)(2,1)S(1)}, u32[]{:S(2)}, u32[]{:S(2)}) collective-permute-start(bf16[4,8,2048]{2,1,0:T(8,128)(2,1)S(1)} %finish.3.refs_0_), channel_id=1, source_target_pairs={{0,2},{1,5},{2,0},{3,7},{4,6},{5,1},{6,4},{7,3},{8,10},{9,13},{10,... | collective-permute-start | bytes 393224 | tf_op jit(solution)/shard_map/ppermute | solution.py:230
  42.1 2.9 %collective-permute-done.6.refs_1_ = bf16[4,136,128]{2,1,0:T(8,128)(2,1)S(1)} collective-permute-done((bf16[4,136,128]{2,1,0:T(8,128)(2,1)S(1)}, bf16[4,136,128]{2,1,0:T(8,128)(2,1)S(1)}, u32[]{:S(2)}, u32[]{:S(2)}) %collective-permute-start.6) | collective-permute-done | bytes 139296 | tf_op jit(solution)/shard_map/ppermute | solution.py:236
  45.3 2.4 %collective-permute-start.20 = (bf16[4,8,2048]{2,1,0:T(8,128)(2,1)S(1)}, bf16[4,8,2048]{2,1,0:T(8,128)(2,1)S(1)}, u32[]{:S(2)}, u32[]{:S(2)}) collective-permute-start(bf16[4,8,2048]{2,1,0:T(8,128)(2,1)S(1)} %finish.3.refs_0_), channel_id=1, source_target_pairs={{0,4},{1,3},{2,6},{3,1},{4,0},{5,7},{6,2},{7,5},{8,12},{9,11},{10,... | collective-permute-start | bytes 393224 | tf_op jit(solution)/shard_map/ppermute | solution.py:230
  47.8 1.9 %collective-permute-start.21 = (bf16[4,8,2048]{2,1,0:T(8,128)(2,1)S(1)}, bf16[4,8,2048]{2,1,0:T(8,128)(2,1)S(1)}, u32[]{:S(2)}, u32[]{:S(2)}) collective-permute-start(bf16[4,8,2048]{2,1,0:T(8,128)(2,1)S(1)} %collective-permute-done.19.refs_1_), channel_id=1, source_target_pairs={{0,4},{1,3},{2,6},{3,1},{4,0},{5,7},{6,2},{7,5},{8,12},{9,11},{10,... | collective-permute-start | bytes 393224 | tf_op jit(solution)/shard_map/ppermute | solution.py:230
  49.8 0.9 %collective-permute-done.10.refs_9_ = bf16[4,8,2048]{2,1,0:T(8,128)(2,1)S(1)} collective-permute-done((bf16[4,8,2048]{2,1,0:T(8,128)(2,1)S(1)}, bf16[4,8,2048]{2,1,0:T(8,128)(2,1)S(1)}, u32[]{:S(2)}, u32[]{:S(2)}) %collective-permute-start.10) | collective-permute-done | bytes 131104 | tf_op jit(solution)/shard_map/ppermute | solution.py:230
  50.6 2.0 %collective-permute-start.12 = (bf16[4,8,2048]{2,1,0:T(8,128)(2,1)S(1)}, bf16[4,8,2048]{2,1,0:T(8,128)(2,1)S(1)}, u32[]{:S(2)}, u32[]{:S(2)}) collective-permute-start(bf16[4,8,2048]{2,1,0:T(8,128)(2,1)S(1)} %collective-permute-done.10.refs_9_), channel_id=1, source_target_pairs={{0,4},{1,3},{2,6},{3,1},{4,0},{5,7},{6,2},{7,5},{8,12},{9,11},{10,... | collective-permute-start | bytes 393224 | tf_op jit(solution)/shard_map/ppermute | solution.py:230
  52.7 0.4 collective-permute-start.24
  53.1 1.0 %collective-permute-done.21.refs_3_ = bf16[4,8,2048]{2,1,0:T(8,128)(2,1)S(1)} collective-permute-done((bf16[4,8,2048]{2,1,0:T(8,128)(2,1)S(1)}, bf16[4,8,2048]{2,1,0:T(8,128)(2,1)S(1)}, u32[]{:S(2)}, u32[]{:S(2)}) %collective-permute-start.21) | collective-permute-done | bytes 131104 | tf_op jit(solution)/shard_map/ppermute | solution.py:230
  54.1 0.5 collective-permute-start.7
  54.6 1.0 %collective-permute-done.12.refs_11_ = bf16[4,8,2048]{2,1,0:T(8,128)(2,1)S(1)} collective-permute-done((bf16[4,8,2048]{2,1,0:T(8,128)(2,1)S(1)}, bf16[4,8,2048]{2,1,0:T(8,128)(2,1)S(1)}, u32[]{:S(2)}, u32[]{:S(2)}) %collective-permute-start.12) | collective-permute-done | bytes 131104 | tf_op jit(solution)/shard_map/ppermute | solution.py:230
  55.6 0.5 collective-permute-start.9
  56.2 1.5 %project.2.refs_4_ = f32[128,512]{1,0:T(8,128)S(1)} custom-call(s32[18]{0:T(128)S(1)} %pad_add_fusion.meta, bf16[8192,512]{1,0:T(8,128)(2,1)S(1)} %bitcast.6, bf16[4,8,2048]{2,1,0:T(8,128)(2,1)S(1)} %finish.3.refs_0_, bf16[4,8,2048]{2,1,0:T(8,128)(2,1)S(1)} %collective-permute-done.19.refs_1_, bf16[4,8,2048]{2,1,0:T(8,128)(2,1)S(1)} %collective-permute-done.20.refs_2_, ...), custom_call_target="tpu_custom_call" | custom-call | flops 805306368 | bytes 6291456 | tf_op jit(solution)/shard_map/project/pallas_call | solution.py:348
  57.8 1.7 %project.3 = f32[128,512]{1,0:T(8,128)} custom-call(s32[18]{0:T(128)S(1)} %pad_add_fusion.meta, bf16[8192,512]{1,0:T(8,128)(2,1)S(1)} %bitcast.6, bf16[4,8,2048]{2,1,0:T(8,128)(2,1)S(1)} %collective-permute-done.7.refs_0_, bf16[4,8,2048]{2,1,0:T(8,128)(2,1)S(1)} %collective-permute-done.9.refs_1_, bf16[4,8,2048]{2,1,0:T(8,128)(2,1)S(1)} %collective-permute-done.11.refs_2_, ...), custom_call_target="tpu_custom_call" | custom-call | flops 268435456 | bytes 2097152 | tf_op jit(solution)/shard_map/project/pallas_call | solution.py:348
  (41 shorter events, 1.2 us)
Async XLA Ops:
  0.7 4.7 %copy-start = (bf16[128,64,128]{2,1,0:T(8,128)(2,1)S(1)}, bf16[128,64,128]{2,1,0:T(8,128)(2,1)}, u32[]{:S(2)}) copy-start(bf16[128,64,128]{2,1,0:T(8,128)(2,1)} %q_ref.3) | copy-start | bytes 6291460
  4.0 5.1 %collective-permute-start = (bf16[16,136,128]{2,1,0:T(8,128)(2,1)S(1)}, bf16[16,136,128]{2,1,0:T(8,128)(2,1)S(1)}, u32[]{:S(2)}, u32[]{:S(2)}) collective-permute-start(bf16[16,136,128]{2,1,0:T(8,128)(2,1)S(1)} %get-tuple-element.31), channel_id=1, source_target_pairs={{0,1},{1,0},{2,3},{3,2},{4,5},{5,4},{6,7},{7,6},{8,9},{9,8},{10,11... | collective-permute-start | bytes 1671176 | tf_op jit(solution)/shard_map/ppermute | solution.py:224
  5.4 50.7 %slice-start = ((s8[8388608]{0:T(1024)(128)(4,1)}), s8[4194304]{0:T(1024)(128)(4,1)S(1)}, s32[]{:S(2)}) async-start(s8[8388608]{0:T(1024)(128)(4,1)} %bitcast.5), calls=%async_computation | async-start | bytes 8388608
  7.8 10.1 %collective-permute-start.1 = (bf16[16,136,128]{2,1,0:T(8,128)(2,1)S(1)}, bf16[16,136,128]{2,1,0:T(8,128)(2,1)S(1)}, u32[]{:S(2)}, u32[]{:S(2)}) collective-permute-start(bf16[16,136,128]{2,1,0:T(8,128)(2,1)S(1)} %get-tuple-element.37), channel_id=1, source_target_pairs={{0,1},{1,0},{2,3},{3,2},{4,5},{5,4},{6,7},{7,6},{8,9},{9,8},{10,11... | collective-permute-start | bytes 1671176 | tf_op jit(solution)/shard_map/ppermute | solution.py:224
  9.1 47.1 %slice-start.1 = ((s8[8388608]{0:T(1024)(128)(4,1)}), s8[4194304]{0:T(1024)(128)(4,1)S(1)}, s32[]{:S(2)}) async-start(s8[8388608]{0:T(1024)(128)(4,1)} %bitcast.5), calls=%async_computation.1 | async-start | bytes 8388608
  10.0 13.5 %collective-permute-start.14 = (bf16[4,136,128]{2,1,0:T(8,128)(2,1)S(1)}, bf16[4,136,128]{2,1,0:T(8,128)(2,1)S(1)}, u32[]{:S(2)}, u32[]{:S(2)}) collective-permute-start(bf16[4,136,128]{2,1,0:T(8,128)(2,1)S(1)} %get-tuple-element.48), channel_id=1, source_target_pairs={{0,2},{1,5},{2,0},{3,7},{4,6},{5,1},{6,4},{7,3},{8,10},{9,13},{10,... | collective-permute-start | bytes 417800 | tf_op jit(solution)/shard_map/ppermute | solution.py:230
  14.6 8.9 %collective-permute-start.15 = (bf16[4,136,128]{2,1,0:T(8,128)(2,1)S(1)}, bf16[4,136,128]{2,1,0:T(8,128)(2,1)S(1)}, u32[]{:S(2)}, u32[]{:S(2)}) collective-permute-start(bf16[4,136,128]{2,1,0:T(8,128)(2,1)S(1)} %get-tuple-element.49), channel_id=1, source_target_pairs={{0,4},{1,3},{2,6},{3,1},{4,0},{5,7},{6,2},{7,5},{8,12},{9,11},{10,... | collective-permute-start | bytes 417800 | tf_op jit(solution)/shard_map/ppermute | solution.py:230
  16.1 7.4 %collective-permute-start.16 = (bf16[4,136,128]{2,1,0:T(8,128)(2,1)S(1)}, bf16[4,136,128]{2,1,0:T(8,128)(2,1)S(1)}, u32[]{:S(2)}, u32[]{:S(2)}) collective-permute-start(bf16[4,136,128]{2,1,0:T(8,128)(2,1)S(1)} %get-tuple-element.50), channel_id=1, source_target_pairs={{0,6},{1,7},{2,4},{3,5},{4,2},{5,3},{6,0},{7,1},{8,14},{9,15},{10,... | collective-permute-start | bytes 417800 | tf_op jit(solution)/shard_map/ppermute | solution.py:230
  18.7 7.7 %collective-permute-start.2 = (bf16[4,136,128]{2,1,0:T(8,128)(2,1)S(1)}, bf16[4,136,128]{2,1,0:T(8,128)(2,1)S(1)}, u32[]{:S(2)}, u32[]{:S(2)}) collective-permute-start(bf16[4,136,128]{2,1,0:T(8,128)(2,1)S(1)} %get-tuple-element.44), channel_id=1, source_target_pairs={{0,2},{1,5},{2,0},{3,7},{4,6},{5,1},{6,4},{7,3},{8,10},{9,13},{10,... | collective-permute-start | bytes 417800 | tf_op jit(solution)/shard_map/ppermute | solution.py:230
  22.0 7.7 %collective-permute-start.3 = (bf16[4,136,128]{2,1,0:T(8,128)(2,1)S(1)}, bf16[4,136,128]{2,1,0:T(8,128)(2,1)S(1)}, u32[]{:S(2)}, u32[]{:S(2)}) collective-permute-start(bf16[4,136,128]{2,1,0:T(8,128)(2,1)S(1)} %get-tuple-element.45), channel_id=1, source_target_pairs={{0,4},{1,3},{2,6},{3,1},{4,0},{5,7},{6,2},{7,5},{8,12},{9,11},{10,... | collective-permute-start | bytes 417800 | tf_op jit(solution)/shard_map/ppermute | solution.py:230
  23.5 6.2 %collective-permute-start.4 = (bf16[4,136,128]{2,1,0:T(8,128)(2,1)S(1)}, bf16[4,136,128]{2,1,0:T(8,128)(2,1)S(1)}, u32[]{:S(2)}, u32[]{:S(2)}) collective-permute-start(bf16[4,136,128]{2,1,0:T(8,128)(2,1)S(1)} %get-tuple-element.46), channel_id=1, source_target_pairs={{0,6},{1,7},{2,4},{3,5},{4,2},{5,3},{6,0},{7,1},{8,14},{9,15},{10,... | collective-permute-start | bytes 417800 | tf_op jit(solution)/shard_map/ppermute | solution.py:230
  23.7 6.2 %collective-permute-start.17 = (bf16[4,136,128]{2,1,0:T(8,128)(2,1)S(1)}, bf16[4,136,128]{2,1,0:T(8,128)(2,1)S(1)}, u32[]{:S(2)}, u32[]{:S(2)}) collective-permute-start(bf16[4,136,128]{2,1,0:T(8,128)(2,1)S(1)} %merge_chips.6.refs_0_), channel_id=1, source_target_pairs={{0,8},{1,17},{2,10},{3,19},{4,12},{5,21},{6,14},{7,23},{8,0},{9,25... | collective-permute-start | bytes 417800 | tf_op jit(solution)/shard_map/ppermute | solution.py:236
  29.8 7.6 %collective-permute-start.5 = (bf16[4,136,128]{2,1,0:T(8,128)(2,1)S(1)}, bf16[4,136,128]{2,1,0:T(8,128)(2,1)S(1)}, u32[]{:S(2)}, u32[]{:S(2)}) collective-permute-start(bf16[4,136,128]{2,1,0:T(8,128)(2,1)S(1)} %merge_chips.4.refs_0_), channel_id=1, source_target_pairs={{0,8},{1,17},{2,10},{3,19},{4,12},{5,21},{6,14},{7,23},{8,0},{9,25... | collective-permute-start | bytes 417800 | tf_op jit(solution)/shard_map/ppermute | solution.py:236
  30.0 9.6 %collective-permute-start.18 = (bf16[4,136,128]{2,1,0:T(8,128)(2,1)S(1)}, bf16[4,136,128]{2,1,0:T(8,128)(2,1)S(1)}, u32[]{:S(2)}, u32[]{:S(2)}) collective-permute-start(bf16[4,136,128]{2,1,0:T(8,128)(2,1)S(1)} %merge_chips.7.refs_0_), channel_id=1, source_target_pairs={{0,16},{1,9},{2,18},{3,11},{4,20},{5,13},{6,22},{7,15},{8,24},{9,1... | collective-permute-start | bytes 417800 | tf_op jit(solution)/shard_map/ppermute | solution.py:236
  37.5 7.5 %collective-permute-start.6 = (bf16[4,136,128]{2,1,0:T(8,128)(2,1)S(1)}, bf16[4,136,128]{2,1,0:T(8,128)(2,1)S(1)}, u32[]{:S(2)}, u32[]{:S(2)}) collective-permute-start(bf16[4,136,128]{2,1,0:T(8,128)(2,1)S(1)} %merge_chips.5.refs_0_), channel_id=1, source_target_pairs={{0,16},{1,9},{2,18},{3,11},{4,20},{5,13},{6,22},{7,15},{8,24},{9,1... | collective-permute-start | bytes 417800 | tf_op jit(solution)/shard_map/ppermute | solution.py:236
  39.8 8.0 %collective-permute-start.19 = (bf16[4,8,2048]{2,1,0:T(8,128)(2,1)S(1)}, bf16[4,8,2048]{2,1,0:T(8,128)(2,1)S(1)}, u32[]{:S(2)}, u32[]{:S(2)}) collective-permute-start(bf16[4,8,2048]{2,1,0:T(8,128)(2,1)S(1)} %finish.3.refs_0_), channel_id=1, source_target_pairs={{0,2},{1,5},{2,0},{3,7},{4,6},{5,1},{6,4},{7,3},{8,10},{9,13},{10,... | collective-permute-start | bytes 393224 | tf_op jit(solution)/shard_map/ppermute | solution.py:230
  45.2 5.4 %collective-permute-start.10 = (bf16[4,8,2048]{2,1,0:T(8,128)(2,1)S(1)}, bf16[4,8,2048]{2,1,0:T(8,128)(2,1)S(1)}, u32[]{:S(2)}, u32[]{:S(2)}) collective-permute-start(bf16[4,8,2048]{2,1,0:T(8,128)(2,1)S(1)} %finish.2.refs_8_), channel_id=1, source_target_pairs={{0,2},{1,5},{2,0},{3,7},{4,6},{5,1},{6,4},{7,3},{8,10},{9,13},{10,... | collective-permute-start | bytes 393224 | tf_op jit(solution)/shard_map/ppermute | solution.py:230
  45.3 7.3 %collective-permute-start.20 = (bf16[4,8,2048]{2,1,0:T(8,128)(2,1)S(1)}, bf16[4,8,2048]{2,1,0:T(8,128)(2,1)S(1)}, u32[]{:S(2)}, u32[]{:S(2)}) collective-permute-start(bf16[4,8,2048]{2,1,0:T(8,128)(2,1)S(1)} %finish.3.refs_0_), channel_id=1, source_target_pairs={{0,4},{1,3},{2,6},{3,1},{4,0},{5,7},{6,2},{7,5},{8,12},{9,11},{10,... | collective-permute-start | bytes 393224 | tf_op jit(solution)/shard_map/ppermute | solution.py:230
  47.7 5.0 %collective-permute-start.8 = (bf16[4,8,2048]{2,1,0:T(8,128)(2,1)S(1)}, bf16[4,8,2048]{2,1,0:T(8,128)(2,1)S(1)}, u32[]{:S(2)}, u32[]{:S(2)}) collective-permute-start(bf16[4,8,2048]{2,1,0:T(8,128)(2,1)S(1)} %finish.2.refs_8_), channel_id=1, source_target_pairs={{0,4},{1,3},{2,6},{3,1},{4,0},{5,7},{6,2},{7,5},{8,12},{9,11},{10,... | collective-permute-start | bytes 393224 | tf_op jit(solution)/shard_map/ppermute | solution.py:230
  47.8 6.3 %collective-permute-start.21 = (bf16[4,8,2048]{2,1,0:T(8,128)(2,1)S(1)}, bf16[4,8,2048]{2,1,0:T(8,128)(2,1)S(1)}, u32[]{:S(2)}, u32[]{:S(2)}) collective-permute-start(bf16[4,8,2048]{2,1,0:T(8,128)(2,1)S(1)} %collective-permute-done.19.refs_1_), channel_id=1, source_target_pairs={{0,4},{1,3},{2,6},{3,1},{4,0},{5,7},{6,2},{7,5},{8,12},{9,11},{10,... | collective-permute-start | bytes 393224 | tf_op jit(solution)/shard_map/ppermute | solution.py:230
  49.8 4.3 %collective-permute-start.22 = (bf16[4,8,2048]{2,1,0:T(8,128)(2,1)S(1)}, bf16[4,8,2048]{2,1,0:T(8,128)(2,1)S(1)}, u32[]{:S(2)}, u32[]{:S(2)}) collective-permute-start(bf16[4,8,2048]{2,1,0:T(8,128)(2,1)S(1)} %finish.3.refs_0_), channel_id=1, source_target_pairs={{0,1},{1,0},{2,3},{3,2},{4,5},{5,4},{6,7},{7,6},{8,9},{9,8},{10,11... | collective-permute-start | bytes 393224 | tf_op jit(solution)/shard_map/ppermute | solution.py:224
  50.6 5.0 %collective-permute-start.12 = (bf16[4,8,2048]{2,1,0:T(8,128)(2,1)S(1)}, bf16[4,8,2048]{2,1,0:T(8,128)(2,1)S(1)}, u32[]{:S(2)}, u32[]{:S(2)}) collective-permute-start(bf16[4,8,2048]{2,1,0:T(8,128)(2,1)S(1)} %collective-permute-done.10.refs_9_), channel_id=1, source_target_pairs={{0,4},{1,3},{2,6},{3,1},{4,0},{5,7},{6,2},{7,5},{8,12},{9,11},{10,... | collective-permute-start | bytes 393224 | tf_op jit(solution)/shard_map/ppermute | solution.py:230
  52.6 3.0 %collective-permute-start.23 = (bf16[4,8,2048]{2,1,0:T(8,128)(2,1)S(1)}, bf16[4,8,2048]{2,1,0:T(8,128)(2,1)S(1)}, u32[]{:S(2)}, u32[]{:S(2)}) collective-permute-start(bf16[4,8,2048]{2,1,0:T(8,128)(2,1)S(1)} %collective-permute-done.20.refs_2_), channel_id=1, source_target_pairs={{0,1},{1,0},{2,3},{3,2},{4,5},{5,4},{6,7},{7,6},{8,9},{9,8},{10,11... | collective-permute-start | bytes 393224 | tf_op jit(solution)/shard_map/ppermute | solution.py:224
  52.7 3.4 %collective-permute-start.24 = (bf16[4,8,2048]{2,1,0:T(8,128)(2,1)S(1)}, bf16[4,8,2048]{2,1,0:T(8,128)(2,1)S(1)}, u32[]{:S(2)}, u32[]{:S(2)}) collective-permute-start(bf16[4,8,2048]{2,1,0:T(8,128)(2,1)S(1)} %collective-permute-done.19.refs_1_), channel_id=1, source_target_pairs={{0,1},{1,0},{2,3},{3,2},{4,5},{5,4},{6,7},{7,6},{8,9},{9,8},{10,11... | collective-permute-start | bytes 393224 | tf_op jit(solution)/shard_map/ppermute | solution.py:224
  54.1 2.1 %collective-permute-start.25 = (bf16[4,8,2048]{2,1,0:T(8,128)(2,1)S(1)}, bf16[4,8,2048]{2,1,0:T(8,128)(2,1)S(1)}, u32[]{:S(2)}, u32[]{:S(2)}) collective-permute-start(bf16[4,8,2048]{2,1,0:T(8,128)(2,1)S(1)} %collective-permute-done.21.refs_3_), channel_id=1, source_target_pairs={{0,1},{1,0},{2,3},{3,2},{4,5},{5,4},{6,7},{7,6},{8,9},{9,8},{10,11... | collective-permute-start | bytes 393224 | tf_op jit(solution)/shard_map/ppermute | solution.py:224
  54.1 3.6 %collective-permute-start.7 = (bf16[4,8,2048]{2,1,0:T(8,128)(2,1)S(1)}, bf16[4,8,2048]{2,1,0:T(8,128)(2,1)S(1)}, u32[]{:S(2)}, u32[]{:S(2)}) collective-permute-start(bf16[4,8,2048]{2,1,0:T(8,128)(2,1)S(1)} %finish.2.refs_8_), channel_id=1, source_target_pairs={{0,1},{1,0},{2,3},{3,2},{4,5},{5,4},{6,7},{7,6},{8,9},{9,8},{10,11... | collective-permute-start | bytes 393224 | tf_op jit(solution)/shard_map/ppermute | solution.py:224
  55.6 2.2 %collective-permute-start.11 = (bf16[4,8,2048]{2,1,0:T(8,128)(2,1)S(1)}, bf16[4,8,2048]{2,1,0:T(8,128)(2,1)S(1)}, u32[]{:S(2)}, u32[]{:S(2)}) collective-permute-start(bf16[4,8,2048]{2,1,0:T(8,128)(2,1)S(1)} %collective-permute-done.10.refs_9_), channel_id=1, source_target_pairs={{0,1},{1,0},{2,3},{3,2},{4,5},{5,4},{6,7},{7,6},{8,9},{9,8},{10,11... | collective-permute-start | bytes 393224 | tf_op jit(solution)/shard_map/ppermute | solution.py:224
  55.6 2.2 %collective-permute-start.9 = (bf16[4,8,2048]{2,1,0:T(8,128)(2,1)S(1)}, bf16[4,8,2048]{2,1,0:T(8,128)(2,1)S(1)}, u32[]{:S(2)}, u32[]{:S(2)}) collective-permute-start(bf16[4,8,2048]{2,1,0:T(8,128)(2,1)S(1)} %collective-permute-done.8.refs_10_), channel_id=1, source_target_pairs={{0,1},{1,0},{2,3},{3,2},{4,5},{5,4},{6,7},{7,6},{8,9},{9,8},{10,11... | collective-permute-start | bytes 393224 | tf_op jit(solution)/shard_map/ppermute | solution.py:224
  56.1 1.7 %collective-permute-start.13 = (bf16[4,8,2048]{2,1,0:T(8,128)(2,1)S(1)}, bf16[4,8,2048]{2,1,0:T(8,128)(2,1)S(1)}, u32[]{:S(2)}, u32[]{:S(2)}) collective-permute-start(bf16[4,8,2048]{2,1,0:T(8,128)(2,1)S(1)} %collective-permute-done.12.refs_11_), channel_id=1, source_target_pairs={{0,1},{1,0},{2,3},{3,2},{4,5},{5,4},{6,7},{7,6},{8,9},{9,8},{10,11... | collective-permute-start | bytes 393224 | tf_op jit(solution)/shard_map/ppermute | solution.py:224
where the time goes:
time: 59.9 us; the launch traced here: 59.5 us
  starting transfers between devices  30.6 us (51%)
  waiting for transfers between devices  14.9 us (25%)
  Pallas kernels  13.1 us (22%)
  other arithmetic  0.75 us (1%)
    ppermute x12, starting transfers between devices, plane_hop(): return lax.ppermute(value, 'ctx', pairs)  19.8 us
    ppermute x12, waiting for transfers between devices, plane_hop(): return lax.ppermute(value, 'ctx', pairs)  8.24 us
    ppermute x4, waiting for transfers between devices, line_hop(): return lax.ppermute(value, 'ctx', pairs)  6.6 us
    ppermute x4, starting transfers between devices, line_hop(): return lax.ppermute(value, 'ctx', pairs)  6.5 us
    ppermute x10, starting transfers between devices, hop(): return lax.ppermute(value, 'ctx', pairs)  4.31 us
    pallas_call x2, Pallas kernels, attend(): pl.pallas_call(functools.partial(attention_kernel, chunk_roles), in_specs...  3.99 us
    pallas_call x1, Pallas kernels, split_and_attend(): pl.pallas_call(split_kernel, in_specs=[SMEM] + [HBM] * 3, out_specs=[VMEM...  3.27 us
    pallas_call x2, Pallas kernels, project(): pl.pallas_call(functools.partial(project_kernel, terms, bool(more), last)...  3.22 us
  transfers between devices with their start and end apart: 26, of which 8 were waited for; matrix products, arithmetic and copies ran while one was open for 0% of the time, Pallas kernels for 14%

commit v1 on v0

--- a/solution.py
+++ b/solution.py
@@ -362,13 +362,11 @@
     def exchange_plane(parts):
         return [parts[0]] + [plane_hop(parts[j], j) for j in (1, 2, 3)]
 
-    def exchange_line(parts):
-        part = merge_chips(parts)
-        reach = 1
-        while 2 * reach < z_size:
-            part = merge_chips([part, line_hop(part, reach, z_size)])
-            reach *= 2
-        return finish([part, line_hop(part, reach, z_size)])
+    def near(part):
+        return merge_chips([part, line_hop(part, 1, z_size)])
+
+    def far(part):
+        return finish([part, line_hop(part, 2, z_size)])
 
     def gather_plane(attended):
         first, second = plane_hop(attended, 1), plane_hop(attended, 2)
@@ -385,9 +383,15 @@
     parts = merge_cores(kept, next_received)
     parts, first[0] = lax.optimization_barrier((parts, first[0]))
     second = exchange_plane(parts)
-    own = gather_plane(exchange_line(first))
+    part = near(merge_chips(first))
+    next_part = merge_chips(second)
+    part, next_part = lax.optimization_barrier((part, next_part))
+    attended = far(part)
+    next_part = near(next_part)
+    attended, next_part = lax.optimization_barrier((attended, next_part))
+    own = gather_plane(attended)
     other = [hop(own[j], 1) for j in (0, 2, 1, 3)]
-    next_own = gather_plane(exchange_line(second))
+    next_own = gather_plane(far(next_part))
     next_other = [hop(next_own[j], 1) for j in (0, 2, 1, 3)]
     total = project([(0, False), (0, True), (1, False)], own + other + next_own, None)
     return project([(1, True)], next_other, total, last=True)

time: 59.9 us -> 59.3 us (0.990); the launches traced: 59.5 us -> 59.5 us
  starting transfers between devices: 30.6 us -> 24.7 us
  waiting for transfers between devices: 14.9 us -> 18 us
  Pallas kernels: 13.1 us -> 15.9 us
    ppermute x10, starting transfers between devices: 4.31 us -> 1.24 us  [hop(): return lax.ppermute(value, 'ctx', pairs)]
    ppermute x12, starting transfers between devices: 19.8 us -> 16.8 us  [plane_hop(): return lax.ppermute(value, 'ctx', pairs)]
    pallas_call x2, Pallas kernels: 3.99 us -> 5.9 us  [attend(): pl.pallas_call(functools.partial(attention_kernel, chunk_roles), in_specs...]
    ppermute x4, waiting for transfers between devices: 6.6 us -> 8.37 us  [line_hop(): return lax.ppermute(value, 'ctx', pairs)]
    ppermute x12, waiting for transfers between devices: 8.24 us -> 9.56 us  [plane_hop(): return lax.ppermute(value, 'ctx', pairs)]
    pallas_call x1, Pallas kernels: 3.27 us -> 4.16 us  [split_and_attend(): pl.pallas_call(split_kernel, in_specs=[SMEM] + [HBM] * 3, out_specs=[VMEM...]
  transfers between devices with their start and end apart: 26 -> 26, of which waited for: 8 -> 11; matrix products, arithmetic and copies ran while one was open for 0% -> 0% of each run, Pallas kernels for 14% -> 17%
where the time goes in v1:
time: 59.3 us; the launch traced here: 59.5 us
  starting transfers between devices  24.7 us (42%)
  waiting for transfers between devices  18 us (30%)
  Pallas kernels  15.9 us (27%)
  other arithmetic  0.75 us (1%)
    ppermute x12, starting transfers between devices, plane_hop(): return lax.ppermute(value, 'ctx', pairs)  16.8 us
    ppermute x12, waiting for transfers between devices, plane_hop(): return lax.ppermute(value, 'ctx', pairs)  9.56 us
    ppermute x4, waiting for transfers between devices, line_hop(): return lax.ppermute(value, 'ctx', pairs)  8.37 us
    ppermute x4, starting transfers between devices, line_hop(): return lax.ppermute(value, 'ctx', pairs)  6.68 us
    pallas_call x2, Pallas kernels, attend(): pl.pallas_call(functools.partial(attention_kernel, chunk_roles), in_specs...  5.9 us
    pallas_call x1, Pallas kernels, split_and_attend(): pl.pallas_call(split_kernel, in_specs=[SMEM] + [HBM] * 3, out_specs=[VMEM...  4.16 us
    pallas_call x2, Pallas kernels, project(): pl.pallas_call(functools.partial(project_kernel, terms, bool(more), last)...  3.23 us
    pallas_call x2, Pallas kernels, merge_cores(): pl.pallas_call(core_kernel, in_specs=[SMEM] + [VMEM] * 2, out_specs=[VMEM...  1.67 us
  transfers between devices with their start and end apart: 26, of which 11 were waited for; matrix products, arithmetic and copies ran while one was open for 0% of the time, Pallas kernels for 17%

profile of v1, /device:TPU:0, one launch (start us, length us, event | category | flops | bytes accessed | tf_op | source)
XLA Modules:
  0.0 59.5 jit_solution(6745652544330033762)
XLA Ops:
  0.0 0.7 %pad_add_fusion.meta = s32[18]{0:T(128)S(1)} fusion(s32[8]{0:T(128)} %param.10, s32[8]{0:T(128)} %bitcast.9, s32[1]{0:T(128)} %bitcast.1, s32[1]{0:T(128)} %bitcast), kind=kLoop, calls=%fused_computation | loop fusion | flops 54 | bytes 144 | tf_op jit(solution)/shard_map/concatenate | solution.py:260
  0.8 4.2 %split_and_attend.1 = (bf16[4,1024,128]{2,1,0:T(8,128)(2,1)S(1)}, bf16[4,136,1024]{2,1,0:T(8,128)(2,1)S(1)}, bf16[16,136,128]{2,1,0:T(8,128)(2,1)S(1)}) custom-call(s32[18]{0:T(128)S(1)} %pad_add_fusion.meta, bf16[4096,128]{1,0:T(8,128)(2,1)} %bitcast.7, bf16[4096,128]{1,0:T(8,128)(2,1)} %bitcast.8, bf16[128,64,128]{2,1,0:T(8,128)(2,1)} %q_ref.3), custom_call_target="tpu_custom_call" | custom-call | flops 1073741824 | bytes 2097152 | tf_op jit(solution)/shard_map/split_and_attend/pallas_call | solution.py:270
  5.0 3.6 %attend.2 = (bf16[16,136,128]{2,1,0:T(8,128)(2,1)S(1)}, bf16[16,136,128]{2,1,0:T(8,128)(2,1)S(1)}) custom-call(s32[18]{0:T(128)S(1)} %pad_add_fusion.meta, bf16[4,1024,128]{2,1,0:T(8,128)(2,1)S(1)} %get-tuple-element.40.kd, bf16[4,136,1024]{2,1,0:T(8,128)(2,1)S(1)} %get-tuple-element.33.vt, bf16[128,64,128]{2,1,0:T(8,128)(2,1)S(1)} %copy-done), custom_call_target="tpu_custom_call" | custom-call | flops 2147483648 | bytes 1048576 | tf_op jit(solution)/shard_map/attend/pallas_call | solution.py:299
  8.7 0.8 %merge_cores.2 = (bf16[4,136,128]{2,1,0:T(8,128)(2,1)S(1)}, bf16[4,136,128]{2,1,0:T(8,128)(2,1)S(1)}, bf16[4,136,128]{2,1,0:T(8,128)(2,1)S(1)}, bf16[4,136,128]{2,1,0:T(8,128)(2,1)S(1)}) custom-call(s32[18]{0:T(128)S(1)} %pad_add_fusion.meta, bf16[16,136,128]{2,1,0:T(8,128)(2,1)S(1)} %get-tuple-element.34.kept, ...), custom_call_target="tpu_custom_call" | custom-call | tf_op jit(solution)/shard_map/merge_cores/pallas_call | solution.py:314
  9.6 4.4 %collective-permute-start.3 = (bf16[4,136,128]{2,1,0:T(8,128)(2,1)S(1)}, bf16[4,136,128]{2,1,0:T(8,128)(2,1)S(1)}, u32[]{:S(2)}, u32[]{:S(2)}) collective-permute-start(bf16[4,136,128]{2,1,0:T(8,128)(2,1)S(1)} %get-tuple-element.49), channel_id=1, source_target_pairs={{0,4},{1,3},{2,6},{3,1},{4,0},{5,7},{6,2},{7,5},{8,12},{9,11},{10,... | collective-permute-start | bytes 417800 | tf_op jit(solution)/shard_map/ppermute | solution.py:230
  14.1 2.3 %attend.3.kept = bf16[16,136,128]{2,1,0:T(8,128)(2,1)S(1)} custom-call(s32[18]{0:T(128)S(1)} %pad_add_fusion.meta, bf16[4,1024,128]{2,1,0:T(8,128)(2,1)S(1)} %get-tuple-element.40.kd, bf16[4,136,1024]{2,1,0:T(8,128)(2,1)S(1)} %get-tuple-element.33.vt, bf16[128,64,128]{2,1,0:T(8,128)(2,1)S(1)} %copy-done), custom_call_target="tpu_custom_call" | custom-call | flops 1073741824 | bytes 524288 | tf_op jit(solution)/shard_map/attend/pallas_call | solution.py:299
  16.4 0.8 %merge_cores.3 = (bf16[4,136,128]{2,1,0:T(8,128)(2,1)S(1)}, bf16[4,136,128]{2,1,0:T(8,128)(2,1)S(1)}, bf16[4,136,128]{2,1,0:T(8,128)(2,1)S(1)}, bf16[4,136,128]{2,1,0:T(8,128)(2,1)S(1)}) custom-call(s32[18]{0:T(128)S(1)} %pad_add_fusion.meta, bf16[16,136,128]{2,1,0:T(8,128)(2,1)S(1)} %attend.3.kept, bf16[16,136,128]{2,1,0:T(8,128)(2,1)S(1)} %collective-permute-done.1.received), custom_call_target="tpu_custom_call" | custom-call | tf_op jit(solution)/shard_map/merge_cores/pallas_call | solution.py:314
  17.3 3.5 %collective-permute-start.7 = (bf16[4,136,128]{2,1,0:T(8,128)(2,1)S(1)}, bf16[4,136,128]{2,1,0:T(8,128)(2,1)S(1)}, u32[]{:S(2)}, u32[]{:S(2)}) collective-permute-start(bf16[4,136,128]{2,1,0:T(8,128)(2,1)S(1)} %get-tuple-element.53), channel_id=1, source_target_pairs={{0,4},{1,3},{2,6},{3,1},{4,0},{5,7},{6,2},{7,5},{8,12},{9,11},{10,... | collective-permute-start | bytes 417800 | tf_op jit(solution)/shard_map/ppermute | solution.py:230
  21.2 0.3 collective-permute-start.5
  21.5 2.3 %collective-permute-done.6.refs_1_ = bf16[4,136,128]{2,1,0:T(8,128)(2,1)S(1)} collective-permute-done((bf16[4,136,128]{2,1,0:T(8,128)(2,1)S(1)}, bf16[4,136,128]{2,1,0:T(8,128)(2,1)S(1)}, u32[]{:S(2)}, u32[]{:S(2)}) %collective-permute-start.6) | collective-permute-done | bytes 139296 | tf_op jit(solution)/shard_map/ppermute | solution.py:230
  23.7 2.7 %collective-permute-done.7.refs_2_ = bf16[4,136,128]{2,1,0:T(8,128)(2,1)S(1)} collective-permute-done((bf16[4,136,128]{2,1,0:T(8,128)(2,1)S(1)}, bf16[4,136,128]{2,1,0:T(8,128)(2,1)S(1)}, u32[]{:S(2)}, u32[]{:S(2)}) %collective-permute-start.7) | collective-permute-done | bytes 139296 | tf_op jit(solution)/shard_map/ppermute | solution.py:230
  26.4 0.5 collective-permute-done.8.refs_3_
  27.1 4.6 %collective-permute-start.9 = (bf16[4,136,128]{2,1,0:T(8,128)(2,1)S(1)}, bf16[4,136,128]{2,1,0:T(8,128)(2,1)S(1)}, u32[]{:S(2)}, u32[]{:S(2)}) collective-permute-start(bf16[4,136,128]{2,1,0:T(8,128)(2,1)S(1)} %merge_chips.5.refs_0_), channel_id=1, source_target_pairs={{0,16},{1,9},{2,18},{3,11},{4,20},{5,13},{6,22},{7,15},{8,24},{9,1... | collective-permute-start | bytes 417800 | tf_op jit(solution)/shard_map/ppermute | solution.py:236
  31.8 5.3 %collective-permute-done.9.refs_1_ = bf16[4,136,128]{2,1,0:T(8,128)(2,1)S(1)} collective-permute-done((bf16[4,136,128]{2,1,0:T(8,128)(2,1)S(1)}, bf16[4,136,128]{2,1,0:T(8,128)(2,1)S(1)}, u32[]{:S(2)}, u32[]{:S(2)}) %collective-permute-start.9) | collective-permute-done | bytes 139296 | tf_op jit(solution)/shard_map/ppermute | solution.py:236
  37.2 0.2 finish.2.refs_0_
  37.4 0.3 collective-permute-done.10.refs_1_
  37.7 1.7 %collective-permute-start.11 = (bf16[4,136,128]{2,1,0:T(8,128)(2,1)S(1)}, bf16[4,136,128]{2,1,0:T(8,128)(2,1)S(1)}, u32[]{:S(2)}, u32[]{:S(2)}) collective-permute-start(bf16[4,136,128]{2,1,0:T(8,128)(2,1)S(1)} %merge_chips.7.refs_0_), channel_id=1, source_target_pairs={{0,16},{1,9},{2,18},{3,11},{4,20},{5,13},{6,22},{7,15},{8,24},{9,1... | collective-permute-start | bytes 417800 | tf_op jit(solution)/shard_map/ppermute | solution.py:236
  39.4 1.3 %collective-permute-start.19 = (bf16[4,8,2048]{2,1,0:T(8,128)(2,1)S(1)}, bf16[4,8,2048]{2,1,0:T(8,128)(2,1)S(1)}, u32[]{:S(2)}, u32[]{:S(2)}) collective-permute-start(bf16[4,8,2048]{2,1,0:T(8,128)(2,1)S(1)} %finish.2.refs_0_), channel_id=1, source_target_pairs={{0,2},{1,5},{2,0},{3,7},{4,6},{5,1},{6,4},{7,3},{8,10},{9,13},{10,... | collective-permute-start | bytes 393224 | tf_op jit(solution)/shard_map/ppermute | solution.py:230
  40.8 0.7 %collective-permute-start.20 = (bf16[4,8,2048]{2,1,0:T(8,128)(2,1)S(1)}, bf16[4,8,2048]{2,1,0:T(8,128)(2,1)S(1)}, u32[]{:S(2)}, u32[]{:S(2)}) collective-permute-start(bf16[4,8,2048]{2,1,0:T(8,128)(2,1)S(1)} %finish.2.refs_0_), channel_id=1, source_target_pairs={{0,4},{1,3},{2,6},{3,1},{4,0},{5,7},{6,2},{7,5},{8,12},{9,11},{10,... | collective-permute-start | bytes 393224 | tf_op jit(solution)/shard_map/ppermute | solution.py:230
  41.5 2.7 %collective-permute-done.11.refs_1_ = bf16[4,136,128]{2,1,0:T(8,128)(2,1)S(1)} collective-permute-done((bf16[4,136,128]{2,1,0:T(8,128)(2,1)S(1)}, bf16[4,136,128]{2,1,0:T(8,128)(2,1)S(1)}, u32[]{:S(2)}, u32[]{:S(2)}) %collective-permute-start.11) | collective-permute-done | bytes 139296 | tf_op jit(solution)/shard_map/ppermute | solution.py:236
  44.5 3.7 %collective-permute-start.15 = (bf16[4,8,2048]{2,1,0:T(8,128)(2,1)S(1)}, bf16[4,8,2048]{2,1,0:T(8,128)(2,1)S(1)}, u32[]{:S(2)}, u32[]{:S(2)}) collective-permute-start(bf16[4,8,2048]{2,1,0:T(8,128)(2,1)S(1)} %finish.3.refs_8_), channel_id=1, source_target_pairs={{0,2},{1,5},{2,0},{3,7},{4,6},{5,1},{6,4},{7,3},{8,10},{9,13},{10,... | collective-permute-start | bytes 393224 | tf_op jit(solution)/shard_map/ppermute | solution.py:230
  48.1 1.0 %collective-permute-start.21 = (bf16[4,8,2048]{2,1,0:T(8,128)(2,1)S(1)}, bf16[4,8,2048]{2,1,0:T(8,128)(2,1)S(1)}, u32[]{:S(2)}, u32[]{:S(2)}) collective-permute-start(bf16[4,8,2048]{2,1,0:T(8,128)(2,1)S(1)} %collective-permute-done.19.refs_1_), channel_id=1, source_target_pairs={{0,4},{1,3},{2,6},{3,1},{4,0},{5,7},{6,2},{7,5},{8,12},{9,11},{10,... | collective-permute-start | bytes 393224 | tf_op jit(solution)/shard_map/ppermute | solution.py:230
  49.1 0.5 collective-permute-start.24
  49.7 1.0 %collective-permute-start.13 = (bf16[4,8,2048]{2,1,0:T(8,128)(2,1)S(1)}, bf16[4,8,2048]{2,1,0:T(8,128)(2,1)S(1)}, u32[]{:S(2)}, u32[]{:S(2)}) collective-permute-start(bf16[4,8,2048]{2,1,0:T(8,128)(2,1)S(1)} %finish.3.refs_8_), channel_id=1, source_target_pairs={{0,4},{1,3},{2,6},{3,1},{4,0},{5,7},{6,2},{7,5},{8,12},{9,11},{10,... | collective-permute-start | bytes 393224 | tf_op jit(solution)/shard_map/ppermute | solution.py:230
  50.7 0.5 collective-permute-done.15.refs_9_
  51.2 0.9 %collective-permute-start.17 = (bf16[4,8,2048]{2,1,0:T(8,128)(2,1)S(1)}, bf16[4,8,2048]{2,1,0:T(8,128)(2,1)S(1)}, u32[]{:S(2)}, u32[]{:S(2)}) collective-permute-start(bf16[4,8,2048]{2,1,0:T(8,128)(2,1)S(1)} %collective-permute-done.15.refs_9_), channel_id=1, source_target_pairs={{0,4},{1,3},{2,6},{3,1},{4,0},{5,7},{6,2},{7,5},{8,12},{9,11},{10,... | collective-permute-start | bytes 393224 | tf_op jit(solution)/shard_map/ppermute | solution.py:230
  52.2 0.9 %collective-permute-done.21.refs_3_ = bf16[4,8,2048]{2,1,0:T(8,128)(2,1)S(1)} collective-permute-done((bf16[4,8,2048]{2,1,0:T(8,128)(2,1)S(1)}, bf16[4,8,2048]{2,1,0:T(8,128)(2,1)S(1)}, u32[]{:S(2)}, u32[]{:S(2)}) %collective-permute-start.21) | collective-permute-done | bytes 131104 | tf_op jit(solution)/shard_map/ppermute | solution.py:230
  53.1 0.5 collective-permute-start.12
  53.7 0.9 %collective-permute-done.13.refs_10_ = bf16[4,8,2048]{2,1,0:T(8,128)(2,1)S(1)} collective-permute-done((bf16[4,8,2048]{2,1,0:T(8,128)(2,1)S(1)}, bf16[4,8,2048]{2,1,0:T(8,128)(2,1)S(1)}, u32[]{:S(2)}, u32[]{:S(2)}) %collective-permute-start.13) | collective-permute-done | bytes 131104 | tf_op jit(solution)/shard_map/ppermute | solution.py:230
  54.6 1.6 %collective-permute-done.17.refs_11_ = bf16[4,8,2048]{2,1,0:T(8,128)(2,1)S(1)} collective-permute-done((bf16[4,8,2048]{2,1,0:T(8,128)(2,1)S(1)}, bf16[4,8,2048]{2,1,0:T(8,128)(2,1)S(1)}, u32[]{:S(2)}, u32[]{:S(2)}) %collective-permute-start.17) | collective-permute-done | bytes 131104 | tf_op jit(solution)/shard_map/ppermute | solution.py:230
  56.2 1.5 %project.2.refs_4_ = f32[128,512]{1,0:T(8,128)S(1)} custom-call(s32[18]{0:T(128)S(1)} %pad_add_fusion.meta, bf16[8192,512]{1,0:T(8,128)(2,1)S(1)} %bitcast.6, bf16[4,8,2048]{2,1,0:T(8,128)(2,1)S(1)} %finish.2.refs_0_, bf16[4,8,2048]{2,1,0:T(8,128)(2,1)S(1)} %collective-permute-done.19.refs_1_, bf16[4,8,2048]{2,1,0:T(8,128)(2,1)S(1)} %collective-permute-done.20.refs_2_, ...), custom_call_target="tpu_custom_call" | custom-call | flops 805306368 | bytes 6291456 | tf_op jit(solution)/shard_map/project/pallas_call | solution.py:348
  57.8 1.7 %project.3 = f32[128,512]{1,0:T(8,128)} custom-call(s32[18]{0:T(128)S(1)} %pad_add_fusion.meta, bf16[8192,512]{1,0:T(8,128)(2,1)S(1)} %bitcast.6, bf16[4,8,2048]{2,1,0:T(8,128)(2,1)S(1)} %collective-permute-done.12.refs_0_, bf16[4,8,2048]{2,1,0:T(8,128)(2,1)S(1)} %collective-permute-done.14.refs_1_, bf16[4,8,2048]{2,1,0:T(8,128)(2,1)S(1)} %collective-permute-done.16.refs_2_, ...), custom_call_target="tpu_custom_call" | custom-call | flops 268435456 | bytes 2097152 | tf_op jit(solution)/shard_map/project/pallas_call | solution.py:348
  (41 shorter events, 1.4 us)
Async XLA Ops:
  0.7 4.2 %copy-start = (bf16[128,64,128]{2,1,0:T(8,128)(2,1)S(1)}, bf16[128,64,128]{2,1,0:T(8,128)(2,1)}, u32[]{:S(2)}) copy-start(bf16[128,64,128]{2,1,0:T(8,128)(2,1)} %q_ref.3) | copy-start | bytes 6291460
  4.9 3.8 %collective-permute-start = (bf16[16,136,128]{2,1,0:T(8,128)(2,1)S(1)}, bf16[16,136,128]{2,1,0:T(8,128)(2,1)S(1)}, u32[]{:S(2)}, u32[]{:S(2)}) collective-permute-start(bf16[16,136,128]{2,1,0:T(8,128)(2,1)S(1)} %get-tuple-element.35), channel_id=1, source_target_pairs={{0,1},{1,0},{2,3},{3,2},{4,5},{5,4},{6,7},{7,6},{8,9},{9,8},{10,11... | collective-permute-start | bytes 1671176 | tf_op jit(solution)/shard_map/ppermute | solution.py:224
  5.0 51.2 %slice-start = ((s8[8388608]{0:T(1024)(128)(4,1)}), s8[4194304]{0:T(1024)(128)(4,1)S(1)}, s32[]{:S(2)}) async-start(s8[8388608]{0:T(1024)(128)(4,1)} %bitcast.5), calls=%async_computation | async-start | bytes 8388608
  8.6 7.8 %collective-permute-start.1 = (bf16[16,136,128]{2,1,0:T(8,128)(2,1)S(1)}, bf16[16,136,128]{2,1,0:T(8,128)(2,1)S(1)}, u32[]{:S(2)}, u32[]{:S(2)}) collective-permute-start(bf16[16,136,128]{2,1,0:T(8,128)(2,1)S(1)} %get-tuple-element.41), channel_id=1, source_target_pairs={{0,1},{1,0},{2,3},{3,2},{4,5},{5,4},{6,7},{7,6},{8,9},{9,8},{10,11... | collective-permute-start | bytes 1671176 | tf_op jit(solution)/shard_map/ppermute | solution.py:224
  8.7 47.5 %slice-start.1 = ((s8[8388608]{0:T(1024)(128)(4,1)}), s8[4194304]{0:T(1024)(128)(4,1)S(1)}, s32[]{:S(2)}) async-start(s8[8388608]{0:T(1024)(128)(4,1)} %bitcast.5), calls=%async_computation.1 | async-start | bytes 8388608
  9.6 11.2 %collective-permute-start.2 = (bf16[4,136,128]{2,1,0:T(8,128)(2,1)S(1)}, bf16[4,136,128]{2,1,0:T(8,128)(2,1)S(1)}, u32[]{:S(2)}, u32[]{:S(2)}) collective-permute-start(bf16[4,136,128]{2,1,0:T(8,128)(2,1)S(1)} %get-tuple-element.48), channel_id=1, source_target_pairs={{0,2},{1,5},{2,0},{3,7},{4,6},{5,1},{6,4},{7,3},{8,10},{9,13},{10,... | collective-permute-start | bytes 417800 | tf_op jit(solution)/shard_map/ppermute | solution.py:230
  9.6 11.2 %collective-permute-start.3 = (bf16[4,136,128]{2,1,0:T(8,128)(2,1)S(1)}, bf16[4,136,128]{2,1,0:T(8,128)(2,1)S(1)}, u32[]{:S(2)}, u32[]{:S(2)}) collective-permute-start(bf16[4,136,128]{2,1,0:T(8,128)(2,1)S(1)} %get-tuple-element.49), channel_id=1, source_target_pairs={{0,4},{1,3},{2,6},{3,1},{4,0},{5,7},{6,2},{7,5},{8,12},{9,11},{10,... | collective-permute-start | bytes 417800 | tf_op jit(solution)/shard_map/ppermute | solution.py:230
  14.1 6.9 %collective-permute-start.4 = (bf16[4,136,128]{2,1,0:T(8,128)(2,1)S(1)}, bf16[4,136,128]{2,1,0:T(8,128)(2,1)S(1)}, u32[]{:S(2)}, u32[]{:S(2)}) collective-permute-start(bf16[4,136,128]{2,1,0:T(8,128)(2,1)S(1)} %get-tuple-element.50), channel_id=1, source_target_pairs={{0,6},{1,7},{2,4},{3,5},{4,2},{5,3},{6,0},{7,1},{8,14},{9,15},{10,... | collective-permute-start | bytes 417800 | tf_op jit(solution)/shard_map/ppermute | solution.py:230
  17.2 6.5 %collective-permute-start.6 = (bf16[4,136,128]{2,1,0:T(8,128)(2,1)S(1)}, bf16[4,136,128]{2,1,0:T(8,128)(2,1)S(1)}, u32[]{:S(2)}, u32[]{:S(2)}) collective-permute-start(bf16[4,136,128]{2,1,0:T(8,128)(2,1)S(1)} %get-tuple-element.52), channel_id=1, source_target_pairs={{0,2},{1,5},{2,0},{3,7},{4,6},{5,1},{6,4},{7,3},{8,10},{9,13},{10,... | collective-permute-start | bytes 417800 | tf_op jit(solution)/shard_map/ppermute | solution.py:230
  17.3 9.1 %collective-permute-start.7 = (bf16[4,136,128]{2,1,0:T(8,128)(2,1)S(1)}, bf16[4,136,128]{2,1,0:T(8,128)(2,1)S(1)}, u32[]{:S(2)}, u32[]{:S(2)}) collective-permute-start(bf16[4,136,128]{2,1,0:T(8,128)(2,1)S(1)} %get-tuple-element.53), channel_id=1, source_target_pairs={{0,4},{1,3},{2,6},{3,1},{4,0},{5,7},{6,2},{7,5},{8,12},{9,11},{10,... | collective-permute-start | bytes 417800 | tf_op jit(solution)/shard_map/ppermute | solution.py:230
  20.8 6.1 %collective-permute-start.8 = (bf16[4,136,128]{2,1,0:T(8,128)(2,1)S(1)}, bf16[4,136,128]{2,1,0:T(8,128)(2,1)S(1)}, u32[]{:S(2)}, u32[]{:S(2)}) collective-permute-start(bf16[4,136,128]{2,1,0:T(8,128)(2,1)S(1)} %get-tuple-element.54), channel_id=1, source_target_pairs={{0,6},{1,7},{2,4},{3,5},{4,2},{5,3},{6,0},{7,1},{8,14},{9,15},{10,... | collective-permute-start | bytes 417800 | tf_op jit(solution)/shard_map/ppermute | solution.py:230
  21.2 5.9 %collective-permute-start.5 = (bf16[4,136,128]{2,1,0:T(8,128)(2,1)S(1)}, bf16[4,136,128]{2,1,0:T(8,128)(2,1)S(1)}, u32[]{:S(2)}, u32[]{:S(2)}) collective-permute-start(bf16[4,136,128]{2,1,0:T(8,128)(2,1)S(1)} %merge_chips.4.refs_0_), channel_id=1, source_target_pairs={{0,8},{1,17},{2,10},{3,19},{4,12},{5,21},{6,14},{7,23},{8,0},{9,25... | collective-permute-start | bytes 417800 | tf_op jit(solution)/shard_map/ppermute | solution.py:236
  27.1 10.0 %collective-permute-start.9 = (bf16[4,136,128]{2,1,0:T(8,128)(2,1)S(1)}, bf16[4,136,128]{2,1,0:T(8,128)(2,1)S(1)}, u32[]{:S(2)}, u32[]{:S(2)}) collective-permute-start(bf16[4,136,128]{2,1,0:T(8,128)(2,1)S(1)} %merge_chips.5.refs_0_), channel_id=1, source_target_pairs={{0,16},{1,9},{2,18},{3,11},{4,20},{5,13},{6,22},{7,15},{8,24},{9,1... | collective-permute-start | bytes 417800 | tf_op jit(solution)/shard_map/ppermute | solution.py:236
  31.7 5.9 %collective-permute-start.10 = (bf16[4,136,128]{2,1,0:T(8,128)(2,1)S(1)}, bf16[4,136,128]{2,1,0:T(8,128)(2,1)S(1)}, u32[]{:S(2)}, u32[]{:S(2)}) collective-permute-start(bf16[4,136,128]{2,1,0:T(8,128)(2,1)S(1)} %merge_chips.6.refs_0_), channel_id=1, source_target_pairs={{0,8},{1,17},{2,10},{3,19},{4,12},{5,21},{6,14},{7,23},{8,0},{9,25... | collective-permute-start | bytes 417800 | tf_op jit(solution)/shard_map/ppermute | solution.py:236
  37.7 6.5 %collective-permute-start.11 = (bf16[4,136,128]{2,1,0:T(8,128)(2,1)S(1)}, bf16[4,136,128]{2,1,0:T(8,128)(2,1)S(1)}, u32[]{:S(2)}, u32[]{:S(2)}) collective-permute-start(bf16[4,136,128]{2,1,0:T(8,128)(2,1)S(1)} %merge_chips.7.refs_0_), channel_id=1, source_target_pairs={{0,16},{1,9},{2,18},{3,11},{4,20},{5,13},{6,22},{7,15},{8,24},{9,1... | collective-permute-start | bytes 417800 | tf_op jit(solution)/shard_map/ppermute | solution.py:236
  39.4 8.7 %collective-permute-start.19 = (bf16[4,8,2048]{2,1,0:T(8,128)(2,1)S(1)}, bf16[4,8,2048]{2,1,0:T(8,128)(2,1)S(1)}, u32[]{:S(2)}, u32[]{:S(2)}) collective-permute-start(bf16[4,8,2048]{2,1,0:T(8,128)(2,1)S(1)} %finish.2.refs_0_), channel_id=1, source_target_pairs={{0,2},{1,5},{2,0},{3,7},{4,6},{5,1},{6,4},{7,3},{8,10},{9,13},{10,... | collective-permute-start | bytes 393224 | tf_op jit(solution)/shard_map/ppermute | solution.py:230
  40.8 8.4 %collective-permute-start.20 = (bf16[4,8,2048]{2,1,0:T(8,128)(2,1)S(1)}, bf16[4,8,2048]{2,1,0:T(8,128)(2,1)S(1)}, u32[]{:S(2)}, u32[]{:S(2)}) collective-permute-start(bf16[4,8,2048]{2,1,0:T(8,128)(2,1)S(1)} %finish.2.refs_0_), channel_id=1, source_target_pairs={{0,4},{1,3},{2,6},{3,1},{4,0},{5,7},{6,2},{7,5},{8,12},{9,11},{10,... | collective-permute-start | bytes 393224 | tf_op jit(solution)/shard_map/ppermute | solution.py:230
  41.5 8.2 %collective-permute-start.22 = (bf16[4,8,2048]{2,1,0:T(8,128)(2,1)S(1)}, bf16[4,8,2048]{2,1,0:T(8,128)(2,1)S(1)}, u32[]{:S(2)}, u32[]{:S(2)}) collective-permute-start(bf16[4,8,2048]{2,1,0:T(8,128)(2,1)S(1)} %finish.2.refs_0_), channel_id=1, source_target_pairs={{0,1},{1,0},{2,3},{3,2},{4,5},{5,4},{6,7},{7,6},{8,9},{9,8},{10,11... | collective-permute-start | bytes 393224 | tf_op jit(solution)/shard_map/ppermute | solution.py:224
  44.5 6.8 %collective-permute-start.15 = (bf16[4,8,2048]{2,1,0:T(8,128)(2,1)S(1)}, bf16[4,8,2048]{2,1,0:T(8,128)(2,1)S(1)}, u32[]{:S(2)}, u32[]{:S(2)}) collective-permute-start(bf16[4,8,2048]{2,1,0:T(8,128)(2,1)S(1)} %finish.3.refs_8_), channel_id=1, source_target_pairs={{0,2},{1,5},{2,0},{3,7},{4,6},{5,1},{6,4},{7,3},{8,10},{9,13},{10,... | collective-permute-start | bytes 393224 | tf_op jit(solution)/shard_map/ppermute | solution.py:230
  48.1 5.0 %collective-permute-start.21 = (bf16[4,8,2048]{2,1,0:T(8,128)(2,1)S(1)}, bf16[4,8,2048]{2,1,0:T(8,128)(2,1)S(1)}, u32[]{:S(2)}, u32[]{:S(2)}) collective-permute-start(bf16[4,8,2048]{2,1,0:T(8,128)(2,1)S(1)} %collective-permute-done.19.refs_1_), channel_id=1, source_target_pairs={{0,4},{1,3},{2,6},{3,1},{4,0},{5,7},{6,2},{7,5},{8,12},{9,11},{10,... | collective-permute-start | bytes 393224 | tf_op jit(solution)/shard_map/ppermute | solution.py:230
  49.1 4.0 %collective-permute-start.23 = (bf16[4,8,2048]{2,1,0:T(8,128)(2,1)S(1)}, bf16[4,8,2048]{2,1,0:T(8,128)(2,1)S(1)}, u32[]{:S(2)}, u32[]{:S(2)}) collective-permute-start(bf16[4,8,2048]{2,1,0:T(8,128)(2,1)S(1)} %collective-permute-done.20.refs_2_), channel_id=1, source_target_pairs={{0,1},{1,0},{2,3},{3,2},{4,5},{5,4},{6,7},{7,6},{8,9},{9,8},{10,11... | collective-permute-start | bytes 393224 | tf_op jit(solution)/shard_map/ppermute | solution.py:224
  49.1 4.5 %collective-permute-start.24 = (bf16[4,8,2048]{2,1,0:T(8,128)(2,1)S(1)}, bf16[4,8,2048]{2,1,0:T(8,128)(2,1)S(1)}, u32[]{:S(2)}, u32[]{:S(2)}) collective-permute-start(bf16[4,8,2048]{2,1,0:T(8,128)(2,1)S(1)} %collective-permute-done.19.refs_1_), channel_id=1, source_target_pairs={{0,1},{1,0},{2,3},{3,2},{4,5},{5,4},{6,7},{7,6},{8,9},{9,8},{10,11... | collective-permute-start | bytes 393224 | tf_op jit(solution)/shard_map/ppermute | solution.py:224
  49.7 5.0 %collective-permute-start.13 = (bf16[4,8,2048]{2,1,0:T(8,128)(2,1)S(1)}, bf16[4,8,2048]{2,1,0:T(8,128)(2,1)S(1)}, u32[]{:S(2)}, u32[]{:S(2)}) collective-permute-start(bf16[4,8,2048]{2,1,0:T(8,128)(2,1)S(1)} %finish.3.refs_8_), channel_id=1, source_target_pairs={{0,4},{1,3},{2,6},{3,1},{4,0},{5,7},{6,2},{7,5},{8,12},{9,11},{10,... | collective-permute-start | bytes 393224 | tf_op jit(solution)/shard_map/ppermute | solution.py:230
  51.2 5.0 %collective-permute-start.17 = (bf16[4,8,2048]{2,1,0:T(8,128)(2,1)S(1)}, bf16[4,8,2048]{2,1,0:T(8,128)(2,1)S(1)}, u32[]{:S(2)}, u32[]{:S(2)}) collective-permute-start(bf16[4,8,2048]{2,1,0:T(8,128)(2,1)S(1)} %collective-permute-done.15.refs_9_), channel_id=1, source_target_pairs={{0,4},{1,3},{2,6},{3,1},{4,0},{5,7},{6,2},{7,5},{8,12},{9,11},{10,... | collective-permute-start | bytes 393224 | tf_op jit(solution)/shard_map/ppermute | solution.py:230
  53.1 3.1 %collective-permute-start.25 = (bf16[4,8,2048]{2,1,0:T(8,128)(2,1)S(1)}, bf16[4,8,2048]{2,1,0:T(8,128)(2,1)S(1)}, u32[]{:S(2)}, u32[]{:S(2)}) collective-permute-start(bf16[4,8,2048]{2,1,0:T(8,128)(2,1)S(1)} %collective-permute-done.21.refs_3_), channel_id=1, source_target_pairs={{0,1},{1,0},{2,3},{3,2},{4,5},{5,4},{6,7},{7,6},{8,9},{9,8},{10,11... | collective-permute-start | bytes 393224 | tf_op jit(solution)/shard_map/ppermute | solution.py:224
  53.1 4.6 %collective-permute-start.12 = (bf16[4,8,2048]{2,1,0:T(8,128)(2,1)S(1)}, bf16[4,8,2048]{2,1,0:T(8,128)(2,1)S(1)}, u32[]{:S(2)}, u32[]{:S(2)}) collective-permute-start(bf16[4,8,2048]{2,1,0:T(8,128)(2,1)S(1)} %finish.3.refs_8_), channel_id=1, source_target_pairs={{0,1},{1,0},{2,3},{3,2},{4,5},{5,4},{6,7},{7,6},{8,9},{9,8},{10,11... | collective-permute-start | bytes 393224 | tf_op jit(solution)/shard_map/ppermute | solution.py:224
  53.6 4.1 %collective-permute-start.16 = (bf16[4,8,2048]{2,1,0:T(8,128)(2,1)S(1)}, bf16[4,8,2048]{2,1,0:T(8,128)(2,1)S(1)}, u32[]{:S(2)}, u32[]{:S(2)}) collective-permute-start(bf16[4,8,2048]{2,1,0:T(8,128)(2,1)S(1)} %collective-permute-done.15.refs_9_), channel_id=1, source_target_pairs={{0,1},{1,0},{2,3},{3,2},{4,5},{5,4},{6,7},{7,6},{8,9},{9,8},{10,11... | collective-permute-start | bytes 393224 | tf_op jit(solution)/shard_map/ppermute | solution.py:224
  54.6 3.2 %collective-permute-start.14 = (bf16[4,8,2048]{2,1,0:T(8,128)(2,1)S(1)}, bf16[4,8,2048]{2,1,0:T(8,128)(2,1)S(1)}, u32[]{:S(2)}, u32[]{:S(2)}) collective-permute-start(bf16[4,8,2048]{2,1,0:T(8,128)(2,1)S(1)} %collective-permute-done.13.refs_10_), channel_id=1, source_target_pairs={{0,1},{1,0},{2,3},{3,2},{4,5},{5,4},{6,7},{7,6},{8,9},{9,8},{10,11... | collective-permute-start | bytes 393224 | tf_op jit(solution)/shard_map/ppermute | solution.py:224
  56.2 1.6 %collective-permute-start.18 = (bf16[4,8,2048]{2,1,0:T(8,128)(2,1)S(1)}, bf16[4,8,2048]{2,1,0:T(8,128)(2,1)S(1)}, u32[]{:S(2)}, u32[]{:S(2)}) collective-permute-start(bf16[4,8,2048]{2,1,0:T(8,128)(2,1)S(1)} %collective-permute-done.17.refs_11_), channel_id=1, source_target_pairs={{0,1},{1,0},{2,3},{3,2},{4,5},{5,4},{6,7},{7,6},{8,9},{9,8},{10,11... | collective-permute-start | bytes 393224 | tf_op jit(solution)/shard_map/ppermute | solution.py:224

commit v2 on v0

--- a/solution.py
+++ b/solution.py
@@ -25,17 +25,14 @@
     return out.astype(bf16), stats.astype(bf16)
 
 
-def active_count(meta):
-    block_count = (meta.shape[0] - 2) // 2
-    return sum((meta[2 + block] > 0).astype(jnp.int32) for block in range(block_count))
-
-
-def split_kernel(meta, k_hbm, v_hbm, q_hbm, kd, vt, sent_ref, *scratch):
-    listed, kept_counts, q_ref, k_ref, v_ref, spread, sems = scratch
+def split_kernel(
+    meta, mask_hbm, counts_hbm, k_hbm, v_hbm, q_hbm, kd, vt, sent_ref, active_ref, *scratch
+):
+    mask, counts, listed, kept_counts, q_ref, k_ref, v_ref, spread, sems = scratch
     d = k_hbm.shape[1]
     kv_count = kd.shape[0]
     group_size = q_ref.shape[1]
-    block_count = (meta.shape[0] - 2) // 2
+    block_count = counts.shape[0]
     group = 1 - meta[0]
 
     heads = pl.ds(pl.multiple_of(group * group_size, group_size), group_size)
@@ -43,16 +40,21 @@
         pltpu.make_async_copy(k_hbm, k_ref, sems.at[0]),
         pltpu.make_async_copy(v_hbm, v_ref, sems.at[1]),
         pltpu.make_async_copy(q_hbm.at[:, heads, :], q_ref, sems.at[2]),
+        pltpu.make_async_copy(mask_hbm, mask, sems.at[3]),
+        pltpu.make_async_copy(counts_hbm, counts, sems.at[4]),
     ]
     for copy in copies:
         copy.start()
 
     def note(block, found):
         listed[found] = block
-        kept_counts[found] = meta[2 + block_count + block]
-        return found + (meta[2 + block] > 0).astype(jnp.int32)
-
+        kept_counts[found] = counts[block]
+        return found + (mask[0, block] > 0).astype(jnp.int32)
+
+    copies[3].wait()
+    copies[4].wait()
     active = lax.fori_loop(0, block_count, note, jnp.int32(0))
+    active_ref[0] = active
     place = lax.broadcasted_iota(jnp.int32, (BLK, LANES), 0)
     across = lax.broadcasted_iota(jnp.int32, (STAT, LANES), 1)
 
@@ -93,7 +95,7 @@
     attend_all(active, [(sent_ref, group, lambda: q_ref[...])], kd, vt)
 
 
-def attention_kernel(chunk_roles, meta, kd, vt, q_ref, *outs):
+def attention_kernel(chunk_roles, meta, active_ref, kd, vt, q_ref, *outs):
     group_size = q_ref.shape[1] // kd.shape[0]
     todo = []
     for out, (chunk, is_other) in zip(outs, chunk_roles):
@@ -104,7 +106,7 @@
             return q_ref[:, heads, :]
 
         todo.append((out, group, read))
-    attend_all(active_count(meta), todo, kd, vt)
+    attend_all(active_ref[0], todo, kd, vt)
 
 
 def attend_all(active, todo, kd, vt):
@@ -257,9 +259,7 @@
     tall = d + STAT
     keys = cache_keys.reshape(positions * kv_count, d)
     values = cache_values.reshape(positions * kv_count, d)
-    place = jnp.concatenate(
-        [jnp.stack([core, my_xy]).astype(jnp.int32), block_mask[0], key_counts]
-    )
+    place = jnp.stack([core, my_xy]).astype(jnp.int32)
     kept_in_hbm = functools.partial(pltpu.with_memory_space_constraint, memory_space=pltpu.HBM)
     state = jax.ShapeDtypeStruct((z_size, tall, LANES), bf16)
 
@@ -269,21 +269,24 @@
     def split_and_attend():
         return pl.pallas_call(
             split_kernel,
-            in_specs=[SMEM] + [HBM] * 3,
-            out_specs=[VMEM] * 3,
+            in_specs=[SMEM] + [HBM] * 5,
+            out_specs=[VMEM] * 3 + [SMEM],
             scratch_shapes=[
+                pltpu.SMEM((1, blocks), jnp.int32),
+                pltpu.SMEM((blocks,), jnp.int32),
                 pltpu.SMEM((blocks + 1,), jnp.int32),
                 pltpu.SMEM((blocks + 1,), jnp.int32),
                 pltpu.VMEM((token_count, group_size, d), bf16),
                 pltpu.VMEM((positions * kv_count, d), bf16),
                 pltpu.VMEM((positions * kv_count, d), bf16),
                 pltpu.VMEM((BLK * kv_count, d), f32),
-                pltpu.SemaphoreType.DMA((3,)),
+                pltpu.SemaphoreType.DMA((5,)),
             ],
             out_shape=[
                 jax.ShapeDtypeStruct((kv_count, positions, d), bf16),
                 jax.ShapeDtypeStruct((kv_count, tall, positions), bf16),
                 partial,
+                jax.ShapeDtypeStruct((1,), jnp.int32),
             ],
             compiler_params=pltpu.CompilerParams(vmem_limit_bytes=32 << 20),
             cost_estimate=pl.CostEstimate(
@@ -292,13 +295,13 @@
                 bytes_accessed=4 * positions * d * kv_count,
             ),
             name="split_and_attend",
-        )(place, kept_in_hbm(keys), kept_in_hbm(values), kept_in_hbm(queries))
-
-    def attend(chunk_roles, kd, vt):
+        )(place, *map(kept_in_hbm, (block_mask, key_counts, keys, values, queries)))
+
+    def attend(chunk_roles, kd, vt, active):
         count = len(chunk_roles)
         return pl.pallas_call(
             functools.partial(attention_kernel, chunk_roles),
-            in_specs=[SMEM] + [VMEM] * 3,
+            in_specs=[SMEM] * 2 + [VMEM] * 3,
             out_specs=[VMEM] * count,
             out_shape=[partial] * count,
             compiler_params=pltpu.CompilerParams(vmem_limit_bytes=32 << 20),
@@ -308,7 +311,7 @@
                 bytes_accessed=4 * positions * d * count,
             ),
             name="attend",
-        )(place, kd, vt, queries)
+        )(place, active, kd, vt, queries)
 
     def merge_cores(kept, received):
         return pl.pallas_call(
@@ -374,14 +377,14 @@
         first, second = plane_hop(attended, 1), plane_hop(attended, 2)
         return [attended, first, second, plane_hop(first, 2)]
 
-    kd, vt, sent = split_and_attend()
+    kd, vt, sent, active = split_and_attend()
     received = hop(sent, 1)
-    kept, sent = attend([(0, False), (1, True)], kd, vt)
+    kept, sent = attend([(0, False), (1, True)], kd, vt, active)
     next_received = hop(sent, 1)
     parts = merge_cores(kept, received)
     parts, kd = lax.optimization_barrier((parts, kd))
     first = exchange_plane(parts)
-    (kept,) = attend([(1, False)], kd, vt)
+    (kept,) = attend([(1, False)], kd, vt, active)
     parts = merge_cores(kept, next_received)
     parts, first[0] = lax.optimization_barrier((parts, first[0]))
     second = exchange_plane(parts)

time: 59.9 us -> 60.5 us (1.010)
  Pallas kernels: 13.1 us -> 17.9 us
  starting transfers between devices: 30.6 us -> 26.6 us
  other arithmetic: 0.75 us -> 0.08 us
    ppermute x12, starting transfers between devices: 19.8 us -> 13.7 us  [plane_hop(): return lax.ppermute(value, 'ctx', pairs)]
    ppermute x4, waiting for transfers between devices: 6.6 us -> 11.8 us  [line_hop(): return lax.ppermute(value, 'ctx', pairs)]
    ppermute x4, starting transfers between devices: 6.5 us -> 11.6 us  [line_hop(): return lax.ppermute(value, 'ctx', pairs)]
    ppermute x12, waiting for transfers between devices: 8.24 us -> 3.61 us  [plane_hop(): return lax.ppermute(value, 'ctx', pairs)]
    pallas_call x2, Pallas kernels: 3.99 us -> 7.31 us  [attend(): pl.pallas_call(functools.partial(attention_kernel, chunk_roles), in_specs...]
    ppermute x10, starting transfers between devices: 4.31 us -> 1.24 us  [hop(): return lax.ppermute(value, 'ctx', pairs)]
    pallas_call x1, Pallas kernels: 3.27 us -> 4.69 us  [split_and_attend(): pl.pallas_call(split_kernel, in_specs=[SMEM] + [HBM] * 5, out_specs=[VMEM...]
    concatenate x1 -> x0, other arithmetic: 0.75 us -> none  [fast_body(): jnp.concatenate([jnp.stack([core, my_xy]).astype(jnp.int32), block_mask[0...]
  transfers between devices with their start and end apart: 26 -> 26, of which waited for: 8 -> 7; matrix products, arithmetic and copies ran while one was open for 0% -> 0% of each run, Pallas kernels for 14% -> 19%
where the time goes in v2:
time: 60.5 us; the launch traced here: 60.3 us
  starting transfers between devices  26.6 us (44%)
  Pallas kernels  17.9 us (30%)
  waiting for transfers between devices  15.5 us (26%)
    ppermute x12, starting transfers between devices, plane_hop(): return lax.ppermute(value, 'ctx', pairs)  13.7 us
    ppermute x4, waiting for transfers between devices, line_hop(): return lax.ppermute(value, 'ctx', pairs)  11.8 us
    ppermute x4, starting transfers between devices, line_hop(): return lax.ppermute(value, 'ctx', pairs)  11.6 us
    pallas_call x2, Pallas kernels, attend(): pl.pallas_call(functools.partial(attention_kernel, chunk_roles), in_specs...  7.31 us
    pallas_call x1, Pallas kernels, split_and_attend(): pl.pallas_call(split_kernel, in_specs=[SMEM] + [HBM] * 5, out_specs=[VMEM...  4.69 us
    ppermute x12, waiting for transfers between devices, plane_hop(): return lax.ppermute(value, 'ctx', pairs)  3.61 us
    pallas_call x2, Pallas kernels, project(): pl.pallas_call(functools.partial(project_kernel, terms, bool(more), last)...  3.32 us
    pallas_call x2, Pallas kernels, merge_cores(): pl.pallas_call(core_kernel, in_specs=[SMEM] + [VMEM] * 2, out_specs=[VMEM...  1.68 us
  transfers between devices with their start and end apart: 26, of which 7 were waited for; matrix products, arithmetic and copies ran while one was open for 0% of the time, Pallas kernels for 19%

profile of v2, /device:TPU:0, one launch (start us, length us, event | category | flops | bytes accessed | tf_op | source)
XLA Modules:
  0.0 60.3 jit_solution(11539518436083697827)
XLA Ops:
  0.1 4.7 %split_and_attend.1 = (bf16[4,1024,128]{2,1,0:T(8,128)(2,1)S(1)}, bf16[4,136,1024]{2,1,0:T(8,128)(2,1)S(1)}, bf16[16,136,128]{2,1,0:T(8,128)(2,1)S(1)}, s32[1]{0:T(128)}) custom-call(s32[2]{0:T(128)S(1)} %pad_add_fusion.meta, s32[1,8]{1,0:T(1,128)} %mask_hbm.1, s32[8]{0:T(128)} %counts_hbm.1, bf16[4096,128]{1,0:T(8,128)(2,1)} %bitcast.6, ...), custom_call_target="tpu_custom_call" | custom-call | flops 1073741824 | bytes 2097152 | tf_op jit(solution)/shard_map/split_and_attend/pallas_call | solution.py:270
  4.9 4.4 %attend.2 = (bf16[16,136,128]{2,1,0:T(8,128)(2,1)S(1)}, bf16[16,136,128]{2,1,0:T(8,128)(2,1)S(1)}) custom-call(s32[2]{0:T(128)S(1)} %pad_add_fusion.meta, s32[1]{0:T(128)} %get-tuple-element.29.active_ref, bf16[4,1024,128]{2,1,0:T(8,128)(2,1)S(1)} %get-tuple-element.38.kd, bf16[4,136,1024]{2,1,0:T(8,128)(2,1)S(1)} %get-tuple-element.31.vt, ...), custom_call_target="tpu_custom_call" | custom-call | flops 2147483648 | bytes 1048576 | tf_op jit(solution)/shard_map/attend/pallas_call | solution.py:302
  9.4 0.8 %merge_cores.2 = (bf16[4,136,128]{2,1,0:T(8,128)(2,1)S(1)}, bf16[4,136,128]{2,1,0:T(8,128)(2,1)S(1)}, bf16[4,136,128]{2,1,0:T(8,128)(2,1)S(1)}, bf16[4,136,128]{2,1,0:T(8,128)(2,1)S(1)}) custom-call(s32[2]{0:T(128)S(1)} %pad_add_fusion.meta, bf16[16,136,128]{2,1,0:T(8,128)(2,1)S(1)} %get-tuple-element.32.kept, ...), custom_call_target="tpu_custom_call" | custom-call | tf_op jit(solution)/shard_map/merge_cores/pallas_call | solution.py:317
  10.2 0.8 %collective-permute-start.14 = (bf16[4,136,128]{2,1,0:T(8,128)(2,1)S(1)}, bf16[4,136,128]{2,1,0:T(8,128)(2,1)S(1)}, u32[]{:S(2)}, u32[]{:S(2)}) collective-permute-start(bf16[4,136,128]{2,1,0:T(8,128)(2,1)S(1)} %get-tuple-element.50), channel_id=1, source_target_pairs={{0,2},{1,5},{2,0},{3,7},{4,6},{5,1},{6,4},{7,3},{8,10},{9,13},{10,... | collective-permute-start | bytes 417800 | tf_op jit(solution)/shard_map/ppermute | solution.py:232
  11.1 2.0 %collective-permute-start.15 = (bf16[4,136,128]{2,1,0:T(8,128)(2,1)S(1)}, bf16[4,136,128]{2,1,0:T(8,128)(2,1)S(1)}, u32[]{:S(2)}, u32[]{:S(2)}) collective-permute-start(bf16[4,136,128]{2,1,0:T(8,128)(2,1)S(1)} %get-tuple-element.51), channel_id=1, source_target_pairs={{0,4},{1,3},{2,6},{3,1},{4,0},{5,7},{6,2},{7,5},{8,12},{9,11},{10,... | collective-permute-start | bytes 417800 | tf_op jit(solution)/shard_map/ppermute | solution.py:232
  13.1 0.7 %collective-permute-start.16 = (bf16[4,136,128]{2,1,0:T(8,128)(2,1)S(1)}, bf16[4,136,128]{2,1,0:T(8,128)(2,1)S(1)}, u32[]{:S(2)}, u32[]{:S(2)}) collective-permute-start(bf16[4,136,128]{2,1,0:T(8,128)(2,1)S(1)} %get-tuple-element.52), channel_id=1, source_target_pairs={{0,6},{1,7},{2,4},{3,5},{4,2},{5,3},{6,0},{7,1},{8,14},{9,15},{10,... | collective-permute-start | bytes 417800 | tf_op jit(solution)/shard_map/ppermute | solution.py:232
  13.8 2.9 %attend.3.kept = bf16[16,136,128]{2,1,0:T(8,128)(2,1)S(1)} custom-call(s32[2]{0:T(128)S(1)} %pad_add_fusion.meta, s32[1]{0:T(128)} %get-tuple-element.29.active_ref, bf16[4,1024,128]{2,1,0:T(8,128)(2,1)S(1)} %get-tuple-element.38.kd, bf16[4,136,1024]{2,1,0:T(8,128)(2,1)S(1)} %get-tuple-element.31.vt, bf16[128,64,128]{2,1,0:T(8,128)(2,1)S(1)} %copy-done), custom_call_target="tpu_custom_call" | custom-call | flops 1073741824 | bytes 524288 | tf_op jit(solution)/shard_map/attend/pallas_call | solution.py:302
  16.7 0.8 %merge_cores.3 = (bf16[4,136,128]{2,1,0:T(8,128)(2,1)S(1)}, bf16[4,136,128]{2,1,0:T(8,128)(2,1)S(1)}, bf16[4,136,128]{2,1,0:T(8,128)(2,1)S(1)}, bf16[4,136,128]{2,1,0:T(8,128)(2,1)S(1)}) custom-call(s32[2]{0:T(128)S(1)} %pad_add_fusion.meta, bf16[16,136,128]{2,1,0:T(8,128)(2,1)S(1)} %attend.3.kept, bf16[16,136,128]{2,1,0:T(8,128)(2,1)S(1)} %collective-permute-done.1.received), custom_call_target="tpu_custom_call" | custom-call | tf_op jit(solution)/shard_map/merge_cores/pallas_call | solution.py:317
  17.8 2.0 %collective-permute-start.3 = (bf16[4,136,128]{2,1,0:T(8,128)(2,1)S(1)}, bf16[4,136,128]{2,1,0:T(8,128)(2,1)S(1)}, u32[]{:S(2)}, u32[]{:S(2)}) collective-permute-start(bf16[4,136,128]{2,1,0:T(8,128)(2,1)S(1)} %get-tuple-element.47), channel_id=1, source_target_pairs={{0,4},{1,3},{2,6},{3,1},{4,0},{5,7},{6,2},{7,5},{8,12},{9,11},{10,... | collective-permute-start | bytes 417800 | tf_op jit(solution)/shard_map/ppermute | solution.py:232
  19.8 1.3 %collective-permute-start.4 = (bf16[4,136,128]{2,1,0:T(8,128)(2,1)S(1)}, bf16[4,136,128]{2,1,0:T(8,128)(2,1)S(1)}, u32[]{:S(2)}, u32[]{:S(2)}) collective-permute-start(bf16[4,136,128]{2,1,0:T(8,128)(2,1)S(1)} %get-tuple-element.48), channel_id=1, source_target_pairs={{0,6},{1,7},{2,4},{3,5},{4,2},{5,3},{6,0},{7,1},{8,14},{9,15},{10,... | collective-permute-start | bytes 417800 | tf_op jit(solution)/shard_map/ppermute | solution.py:232
  21.3 5.3 %collective-permute-start.17 = (bf16[4,136,128]{2,1,0:T(8,128)(2,1)S(1)}, bf16[4,136,128]{2,1,0:T(8,128)(2,1)S(1)}, u32[]{:S(2)}, u32[]{:S(2)}) collective-permute-start(bf16[4,136,128]{2,1,0:T(8,128)(2,1)S(1)} %merge_chips.6.refs_0_), channel_id=1, source_target_pairs={{0,8},{1,17},{2,10},{3,19},{4,12},{5,21},{6,14},{7,23},{8,0},{9,25... | collective-permute-start | bytes 417800 | tf_op jit(solution)/shard_map/ppermute | solution.py:238
  26.8 5.8 %collective-permute-start.5 = (bf16[4,136,128]{2,1,0:T(8,128)(2,1)S(1)}, bf16[4,136,128]{2,1,0:T(8,128)(2,1)S(1)}, u32[]{:S(2)}, u32[]{:S(2)}) collective-permute-start(bf16[4,136,128]{2,1,0:T(8,128)(2,1)S(1)} %merge_chips.4.refs_0_), channel_id=1, source_target_pairs={{0,8},{1,17},{2,10},{3,19},{4,12},{5,21},{6,14},{7,23},{8,0},{9,25... | collective-permute-start | bytes 417800 | tf_op jit(solution)/shard_map/ppermute | solution.py:238
  32.7 5.7 %collective-permute-done.5.refs_1_ = bf16[4,136,128]{2,1,0:T(8,128)(2,1)S(1)} collective-permute-done((bf16[4,136,128]{2,1,0:T(8,128)(2,1)S(1)}, bf16[4,136,128]{2,1,0:T(8,128)(2,1)S(1)}, u32[]{:S(2)}, u32[]{:S(2)}) %collective-permute-start.5) | collective-permute-done | bytes 139296 | tf_op jit(solution)/shard_map/ppermute | solution.py:238
  38.5 0.5 collective-permute-start.6
  39.0 1.3 %collective-permute-done.18.refs_1_ = bf16[4,136,128]{2,1,0:T(8,128)(2,1)S(1)} collective-permute-done((bf16[4,136,128]{2,1,0:T(8,128)(2,1)S(1)}, bf16[4,136,128]{2,1,0:T(8,128)(2,1)S(1)}, u32[]{:S(2)}, u32[]{:S(2)}) %collective-permute-start.18) | collective-permute-done | bytes 139296 | tf_op jit(solution)/shard_map/ppermute | solution.py:238
  40.2 0.2 finish.3.refs_0_
  40.5 0.7 %collective-permute-start.19 = (bf16[4,8,2048]{2,1,0:T(8,128)(2,1)S(1)}, bf16[4,8,2048]{2,1,0:T(8,128)(2,1)S(1)}, u32[]{:S(2)}, u32[]{:S(2)}) collective-permute-start(bf16[4,8,2048]{2,1,0:T(8,128)(2,1)S(1)} %finish.3.refs_0_), channel_id=1, source_target_pairs={{0,2},{1,5},{2,0},{3,7},{4,6},{5,1},{6,4},{7,3},{8,10},{9,13},{10,... | collective-permute-start | bytes 393224 | tf_op jit(solution)/shard_map/ppermute | solution.py:232
  41.1 4.9 %collective-permute-done.6.refs_1_ = bf16[4,136,128]{2,1,0:T(8,128)(2,1)S(1)} collective-permute-done((bf16[4,136,128]{2,1,0:T(8,128)(2,1)S(1)}, bf16[4,136,128]{2,1,0:T(8,128)(2,1)S(1)}, u32[]{:S(2)}, u32[]{:S(2)}) %collective-permute-start.6) | collective-permute-done | bytes 139296 | tf_op jit(solution)/shard_map/ppermute | solution.py:238
  46.0 0.2 finish.2.refs_8_
  46.2 0.7 %collective-permute-start.10 = (bf16[4,8,2048]{2,1,0:T(8,128)(2,1)S(1)}, bf16[4,8,2048]{2,1,0:T(8,128)(2,1)S(1)}, u32[]{:S(2)}, u32[]{:S(2)}) collective-permute-start(bf16[4,8,2048]{2,1,0:T(8,128)(2,1)S(1)} %finish.2.refs_8_), channel_id=1, source_target_pairs={{0,2},{1,5},{2,0},{3,7},{4,6},{5,1},{6,4},{7,3},{8,10},{9,13},{10,... | collective-permute-start | bytes 393224 | tf_op jit(solution)/shard_map/ppermute | solution.py:232
  47.0 1.5 %collective-permute-start.20 = (bf16[4,8,2048]{2,1,0:T(8,128)(2,1)S(1)}, bf16[4,8,2048]{2,1,0:T(8,128)(2,1)S(1)}, u32[]{:S(2)}, u32[]{:S(2)}) collective-permute-start(bf16[4,8,2048]{2,1,0:T(8,128)(2,1)S(1)} %finish.3.refs_0_), channel_id=1, source_target_pairs={{0,4},{1,3},{2,6},{3,1},{4,0},{5,7},{6,2},{7,5},{8,12},{9,11},{10,... | collective-permute-start | bytes 393224 | tf_op jit(solution)/shard_map/ppermute | solution.py:232
  48.5 0.5 collective-permute-start.8
  49.0 1.5 %collective-permute-start.21 = (bf16[4,8,2048]{2,1,0:T(8,128)(2,1)S(1)}, bf16[4,8,2048]{2,1,0:T(8,128)(2,1)S(1)}, u32[]{:S(2)}, u32[]{:S(2)}) collective-permute-start(bf16[4,8,2048]{2,1,0:T(8,128)(2,1)S(1)} %collective-permute-done.19.refs_1_), channel_id=1, source_target_pairs={{0,4},{1,3},{2,6},{3,1},{4,0},{5,7},{6,2},{7,5},{8,12},{9,11},{10,... | collective-permute-start | bytes 393224 | tf_op jit(solution)/shard_map/ppermute | solution.py:232
  50.5 0.7 %collective-permute-done.10.refs_9_ = bf16[4,8,2048]{2,1,0:T(8,128)(2,1)S(1)} collective-permute-done((bf16[4,8,2048]{2,1,0:T(8,128)(2,1)S(1)}, bf16[4,8,2048]{2,1,0:T(8,128)(2,1)S(1)}, u32[]{:S(2)}, u32[]{:S(2)}) %collective-permute-start.10) | collective-permute-done | bytes 131104 | tf_op jit(solution)/shard_map/ppermute | solution.py:232
  51.3 1.6 %collective-permute-start.12 = (bf16[4,8,2048]{2,1,0:T(8,128)(2,1)S(1)}, bf16[4,8,2048]{2,1,0:T(8,128)(2,1)S(1)}, u32[]{:S(2)}, u32[]{:S(2)}) collective-permute-start(bf16[4,8,2048]{2,1,0:T(8,128)(2,1)S(1)} %collective-permute-done.10.refs_9_), channel_id=1, source_target_pairs={{0,4},{1,3},{2,6},{3,1},{4,0},{5,7},{6,2},{7,5},{8,12},{9,11},{10,... | collective-permute-start | bytes 393224 | tf_op jit(solution)/shard_map/ppermute | solution.py:232
  52.9 0.6 collective-permute-done.8.refs_10_
  53.5 1.4 %collective-permute-done.21.refs_3_ = bf16[4,8,2048]{2,1,0:T(8,128)(2,1)S(1)} collective-permute-done((bf16[4,8,2048]{2,1,0:T(8,128)(2,1)S(1)}, bf16[4,8,2048]{2,1,0:T(8,128)(2,1)S(1)}, u32[]{:S(2)}, u32[]{:S(2)}) %collective-permute-start.21) | collective-permute-done | bytes 131104 | tf_op jit(solution)/shard_map/ppermute | solution.py:232
  54.9 0.5 collective-permute-start.7
  55.4 0.9 %collective-permute-done.12.refs_11_ = bf16[4,8,2048]{2,1,0:T(8,128)(2,1)S(1)} collective-permute-done((bf16[4,8,2048]{2,1,0:T(8,128)(2,1)S(1)}, bf16[4,8,2048]{2,1,0:T(8,128)(2,1)S(1)}, u32[]{:S(2)}, u32[]{:S(2)}) %collective-permute-start.12) | collective-permute-done | bytes 131104 | tf_op jit(solution)/shard_map/ppermute | solution.py:232
  56.3 0.5 collective-permute-start.9
  56.9 1.6 %project.2.refs_4_ = f32[128,512]{1,0:T(8,128)S(1)} custom-call(s32[2]{0:T(128)S(1)} %pad_add_fusion.meta, bf16[8192,512]{1,0:T(8,128)(2,1)S(1)} %bitcast.5, bf16[4,8,2048]{2,1,0:T(8,128)(2,1)S(1)} %finish.3.refs_0_, bf16[4,8,2048]{2,1,0:T(8,128)(2,1)S(1)} %collective-permute-done.19.refs_1_, bf16[4,8,2048]{2,1,0:T(8,128)(2,1)S(1)} %collective-permute-done.20.refs_2_, ...), custom_call_target="tpu_custom_call" | custom-call | flops 805306368 | bytes 6291456 | tf_op jit(solution)/shard_map/project/pallas_call | solution.py:351
  58.5 1.7 %project.3 = f32[128,512]{1,0:T(8,128)} custom-call(s32[2]{0:T(128)S(1)} %pad_add_fusion.meta, bf16[8192,512]{1,0:T(8,128)(2,1)S(1)} %bitcast.5, bf16[4,8,2048]{2,1,0:T(8,128)(2,1)S(1)} %collective-permute-done.7.refs_0_, bf16[4,8,2048]{2,1,0:T(8,128)(2,1)S(1)} %collective-permute-done.9.refs_1_, bf16[4,8,2048]{2,1,0:T(8,128)(2,1)S(1)} %collective-permute-done.11.refs_2_, ...), custom_call_target="tpu_custom_call" | custom-call | flops 268435456 | bytes 2097152 | tf_op jit(solution)/shard_map/project/pallas_call | solution.py:351
  (41 shorter events, 1.1 us)
Async XLA Ops:
  0.1 4.8 %copy-start = (bf16[128,64,128]{2,1,0:T(8,128)(2,1)S(1)}, bf16[128,64,128]{2,1,0:T(8,128)(2,1)}, u32[]{:S(2)}) copy-start(bf16[128,64,128]{2,1,0:T(8,128)(2,1)} %q_ref.3) | copy-start | bytes 6291460
  4.8 4.6 %collective-permute-start = (bf16[16,136,128]{2,1,0:T(8,128)(2,1)S(1)}, bf16[16,136,128]{2,1,0:T(8,128)(2,1)S(1)}, u32[]{:S(2)}, u32[]{:S(2)}) collective-permute-start(bf16[16,136,128]{2,1,0:T(8,128)(2,1)S(1)} %get-tuple-element.33), channel_id=1, source_target_pairs={{0,1},{1,0},{2,3},{3,2},{4,5},{5,4},{6,7},{7,6},{8,9},{9,8},{10,11... | collective-permute-start | bytes 1671176 | tf_op jit(solution)/shard_map/ppermute | solution.py:226
  4.9 52.0 %slice-start = ((s8[8388608]{0:T(1024)(128)(4,1)}), s8[4194304]{0:T(1024)(128)(4,1)S(1)}, s32[]{:S(2)}) async-start(s8[8388608]{0:T(1024)(128)(4,1)} %bitcast.4), calls=%async_computation | async-start | bytes 8388608
  9.3 7.4 %collective-permute-start.1 = (bf16[16,136,128]{2,1,0:T(8,128)(2,1)S(1)}, bf16[16,136,128]{2,1,0:T(8,128)(2,1)S(1)}, u32[]{:S(2)}, u32[]{:S(2)}) collective-permute-start(bf16[16,136,128]{2,1,0:T(8,128)(2,1)S(1)} %get-tuple-element.39), channel_id=1, source_target_pairs={{0,1},{1,0},{2,3},{3,2},{4,5},{5,4},{6,7},{7,6},{8,9},{9,8},{10,11... | collective-permute-start | bytes 1671176 | tf_op jit(solution)/shard_map/ppermute | solution.py:226
  9.4 47.5 %slice-start.1 = ((s8[8388608]{0:T(1024)(128)(4,1)}), s8[4194304]{0:T(1024)(128)(4,1)S(1)}, s32[]{:S(2)}) async-start(s8[8388608]{0:T(1024)(128)(4,1)} %bitcast.4), calls=%async_computation.1 | async-start | bytes 8388608
  10.2 9.6 %collective-permute-start.14 = (bf16[4,136,128]{2,1,0:T(8,128)(2,1)S(1)}, bf16[4,136,128]{2,1,0:T(8,128)(2,1)S(1)}, u32[]{:S(2)}, u32[]{:S(2)}) collective-permute-start(bf16[4,136,128]{2,1,0:T(8,128)(2,1)S(1)} %get-tuple-element.50), channel_id=1, source_target_pairs={{0,2},{1,5},{2,0},{3,7},{4,6},{5,1},{6,4},{7,3},{8,10},{9,13},{10,... | collective-permute-start | bytes 417800 | tf_op jit(solution)/shard_map/ppermute | solution.py:232
  11.1 10.1 %collective-permute-start.15 = (bf16[4,136,128]{2,1,0:T(8,128)(2,1)S(1)}, bf16[4,136,128]{2,1,0:T(8,128)(2,1)S(1)}, u32[]{:S(2)}, u32[]{:S(2)}) collective-permute-start(bf16[4,136,128]{2,1,0:T(8,128)(2,1)S(1)} %get-tuple-element.51), channel_id=1, source_target_pairs={{0,4},{1,3},{2,6},{3,1},{4,0},{5,7},{6,2},{7,5},{8,12},{9,11},{10,... | collective-permute-start | bytes 417800 | tf_op jit(solution)/shard_map/ppermute | solution.py:232
  13.1 8.0 %collective-permute-start.16 = (bf16[4,136,128]{2,1,0:T(8,128)(2,1)S(1)}, bf16[4,136,128]{2,1,0:T(8,128)(2,1)S(1)}, u32[]{:S(2)}, u32[]{:S(2)}) collective-permute-start(bf16[4,136,128]{2,1,0:T(8,128)(2,1)S(1)} %get-tuple-element.52), channel_id=1, source_target_pairs={{0,6},{1,7},{2,4},{3,5},{4,2},{5,3},{6,0},{7,1},{8,14},{9,15},{10,... | collective-permute-start | bytes 417800 | tf_op jit(solution)/shard_map/ppermute | solution.py:232
  17.6 9.0 %collective-permute-start.2 = (bf16[4,136,128]{2,1,0:T(8,128)(2,1)S(1)}, bf16[4,136,128]{2,1,0:T(8,128)(2,1)S(1)}, u32[]{:S(2)}, u32[]{:S(2)}) collective-permute-start(bf16[4,136,128]{2,1,0:T(8,128)(2,1)S(1)} %get-tuple-element.46), channel_id=1, source_target_pairs={{0,2},{1,5},{2,0},{3,7},{4,6},{5,1},{6,4},{7,3},{8,10},{9,13},{10,... | collective-permute-start | bytes 417800 | tf_op jit(solution)/shard_map/ppermute | solution.py:232
  17.8 8.8 %collective-permute-start.3 = (bf16[4,136,128]{2,1,0:T(8,128)(2,1)S(1)}, bf16[4,136,128]{2,1,0:T(8,128)(2,1)S(1)}, u32[]{:S(2)}, u32[]{:S(2)}) collective-permute-start(bf16[4,136,128]{2,1,0:T(8,128)(2,1)S(1)} %get-tuple-element.47), channel_id=1, source_target_pairs={{0,4},{1,3},{2,6},{3,1},{4,0},{5,7},{6,2},{7,5},{8,12},{9,11},{10,... | collective-permute-start | bytes 417800 | tf_op jit(solution)/shard_map/ppermute | solution.py:232
  19.8 6.8 %collective-permute-start.4 = (bf16[4,136,128]{2,1,0:T(8,128)(2,1)S(1)}, bf16[4,136,128]{2,1,0:T(8,128)(2,1)S(1)}, u32[]{:S(2)}, u32[]{:S(2)}) collective-permute-start(bf16[4,136,128]{2,1,0:T(8,128)(2,1)S(1)} %get-tuple-element.48), channel_id=1, source_target_pairs={{0,6},{1,7},{2,4},{3,5},{4,2},{5,3},{6,0},{7,1},{8,14},{9,15},{10,... | collective-permute-start | bytes 417800 | tf_op jit(solution)/shard_map/ppermute | solution.py:232
  21.3 11.2 %collective-permute-start.17 = (bf16[4,136,128]{2,1,0:T(8,128)(2,1)S(1)}, bf16[4,136,128]{2,1,0:T(8,128)(2,1)S(1)}, u32[]{:S(2)}, u32[]{:S(2)}) collective-permute-start(bf16[4,136,128]{2,1,0:T(8,128)(2,1)S(1)} %merge_chips.6.refs_0_), channel_id=1, source_target_pairs={{0,8},{1,17},{2,10},{3,19},{4,12},{5,21},{6,14},{7,23},{8,0},{9,25... | collective-permute-start | bytes 417800 | tf_op jit(solution)/shard_map/ppermute | solution.py:238
  26.8 11.6 %collective-permute-start.5 = (bf16[4,136,128]{2,1,0:T(8,128)(2,1)S(1)}, bf16[4,136,128]{2,1,0:T(8,128)(2,1)S(1)}, u32[]{:S(2)}, u32[]{:S(2)}) collective-permute-start(bf16[4,136,128]{2,1,0:T(8,128)(2,1)S(1)} %merge_chips.4.refs_0_), channel_id=1, source_target_pairs={{0,8},{1,17},{2,10},{3,19},{4,12},{5,21},{6,14},{7,23},{8,0},{9,25... | collective-permute-start | bytes 417800 | tf_op jit(solution)/shard_map/ppermute | solution.py:238
  32.6 7.6 %collective-permute-start.18 = (bf16[4,136,128]{2,1,0:T(8,128)(2,1)S(1)}, bf16[4,136,128]{2,1,0:T(8,128)(2,1)S(1)}, u32[]{:S(2)}, u32[]{:S(2)}) collective-permute-start(bf16[4,136,128]{2,1,0:T(8,128)(2,1)S(1)} %merge_chips.7.refs_0_), channel_id=1, source_target_pairs={{0,16},{1,9},{2,18},{3,11},{4,20},{5,13},{6,22},{7,15},{8,24},{9,1... | collective-permute-start | bytes 417800 | tf_op jit(solution)/shard_map/ppermute | solution.py:238
  38.5 7.5 %collective-permute-start.6 = (bf16[4,136,128]{2,1,0:T(8,128)(2,1)S(1)}, bf16[4,136,128]{2,1,0:T(8,128)(2,1)S(1)}, u32[]{:S(2)}, u32[]{:S(2)}) collective-permute-start(bf16[4,136,128]{2,1,0:T(8,128)(2,1)S(1)} %merge_chips.5.refs_0_), channel_id=1, source_target_pairs={{0,16},{1,9},{2,18},{3,11},{4,20},{5,13},{6,22},{7,15},{8,24},{9,1... | collective-permute-start | bytes 417800 | tf_op jit(solution)/shard_map/ppermute | solution.py:238
  40.5 8.5 %collective-permute-start.19 = (bf16[4,8,2048]{2,1,0:T(8,128)(2,1)S(1)}, bf16[4,8,2048]{2,1,0:T(8,128)(2,1)S(1)}, u32[]{:S(2)}, u32[]{:S(2)}) collective-permute-start(bf16[4,8,2048]{2,1,0:T(8,128)(2,1)S(1)} %finish.3.refs_0_), channel_id=1, source_target_pairs={{0,2},{1,5},{2,0},{3,7},{4,6},{5,1},{6,4},{7,3},{8,10},{9,13},{10,... | collective-permute-start | bytes 393224 | tf_op jit(solution)/shard_map/ppermute | solution.py:232
  46.2 5.0 %collective-permute-start.10 = (bf16[4,8,2048]{2,1,0:T(8,128)(2,1)S(1)}, bf16[4,8,2048]{2,1,0:T(8,128)(2,1)S(1)}, u32[]{:S(2)}, u32[]{:S(2)}) collective-permute-start(bf16[4,8,2048]{2,1,0:T(8,128)(2,1)S(1)} %finish.2.refs_8_), channel_id=1, source_target_pairs={{0,2},{1,5},{2,0},{3,7},{4,6},{5,1},{6,4},{7,3},{8,10},{9,13},{10,... | collective-permute-start | bytes 393224 | tf_op jit(solution)/shard_map/ppermute | solution.py:232
  47.0 5.9 %collective-permute-start.20 = (bf16[4,8,2048]{2,1,0:T(8,128)(2,1)S(1)}, bf16[4,8,2048]{2,1,0:T(8,128)(2,1)S(1)}, u32[]{:S(2)}, u32[]{:S(2)}) collective-permute-start(bf16[4,8,2048]{2,1,0:T(8,128)(2,1)S(1)} %finish.3.refs_0_), channel_id=1, source_target_pairs={{0,4},{1,3},{2,6},{3,1},{4,0},{5,7},{6,2},{7,5},{8,12},{9,11},{10,... | collective-permute-start | bytes 393224 | tf_op jit(solution)/shard_map/ppermute | solution.py:232
  48.5 5.0 %collective-permute-start.8 = (bf16[4,8,2048]{2,1,0:T(8,128)(2,1)S(1)}, bf16[4,8,2048]{2,1,0:T(8,128)(2,1)S(1)}, u32[]{:S(2)}, u32[]{:S(2)}) collective-permute-start(bf16[4,8,2048]{2,1,0:T(8,128)(2,1)S(1)} %finish.2.refs_8_), channel_id=1, source_target_pairs={{0,4},{1,3},{2,6},{3,1},{4,0},{5,7},{6,2},{7,5},{8,12},{9,11},{10,... | collective-permute-start | bytes 393224 | tf_op jit(solution)/shard_map/ppermute | solution.py:232
  49.0 5.9 %collective-permute-start.21 = (bf16[4,8,2048]{2,1,0:T(8,128)(2,1)S(1)}, bf16[4,8,2048]{2,1,0:T(8,128)(2,1)S(1)}, u32[]{:S(2)}, u32[]{:S(2)}) collective-permute-start(bf16[4,8,2048]{2,1,0:T(8,128)(2,1)S(1)} %collective-permute-done.19.refs_1_), channel_id=1, source_target_pairs={{0,4},{1,3},{2,6},{3,1},{4,0},{5,7},{6,2},{7,5},{8,12},{9,11},{10,... | collective-permute-start | bytes 393224 | tf_op jit(solution)/shard_map/ppermute | solution.py:232
  50.5 4.3 %collective-permute-start.22 = (bf16[4,8,2048]{2,1,0:T(8,128)(2,1)S(1)}, bf16[4,8,2048]{2,1,0:T(8,128)(2,1)S(1)}, u32[]{:S(2)}, u32[]{:S(2)}) collective-permute-start(bf16[4,8,2048]{2,1,0:T(8,128)(2,1)S(1)} %finish.3.refs_0_), channel_id=1, source_target_pairs={{0,1},{1,0},{2,3},{3,2},{4,5},{5,4},{6,7},{7,6},{8,9},{9,8},{10,11... | collective-permute-start | bytes 393224 | tf_op jit(solution)/shard_map/ppermute | solution.py:226
  51.3 5.0 %collective-permute-start.12 = (bf16[4,8,2048]{2,1,0:T(8,128)(2,1)S(1)}, bf16[4,8,2048]{2,1,0:T(8,128)(2,1)S(1)}, u32[]{:S(2)}, u32[]{:S(2)}) collective-permute-start(bf16[4,8,2048]{2,1,0:T(8,128)(2,1)S(1)} %collective-permute-done.10.refs_9_), channel_id=1, source_target_pairs={{0,4},{1,3},{2,6},{3,1},{4,0},{5,7},{6,2},{7,5},{8,12},{9,11},{10,... | collective-permute-start | bytes 393224 | tf_op jit(solution)/shard_map/ppermute | solution.py:232
  52.9 3.4 %collective-permute-start.23 = (bf16[4,8,2048]{2,1,0:T(8,128)(2,1)S(1)}, bf16[4,8,2048]{2,1,0:T(8,128)(2,1)S(1)}, u32[]{:S(2)}, u32[]{:S(2)}) collective-permute-start(bf16[4,8,2048]{2,1,0:T(8,128)(2,1)S(1)} %collective-permute-done.20.refs_2_), channel_id=1, source_target_pairs={{0,1},{1,0},{2,3},{3,2},{4,5},{5,4},{6,7},{7,6},{8,9},{9,8},{10,11... | collective-permute-start | bytes 393224 | tf_op jit(solution)/shard_map/ppermute | solution.py:226
  53.5 3.3 %collective-permute-start.24 = (bf16[4,8,2048]{2,1,0:T(8,128)(2,1)S(1)}, bf16[4,8,2048]{2,1,0:T(8,128)(2,1)S(1)}, u32[]{:S(2)}, u32[]{:S(2)}) collective-permute-start(bf16[4,8,2048]{2,1,0:T(8,128)(2,1)S(1)} %collective-permute-done.19.refs_1_), channel_id=1, source_target_pairs={{0,1},{1,0},{2,3},{3,2},{4,5},{5,4},{6,7},{7,6},{8,9},{9,8},{10,11... | collective-permute-start | bytes 393224 | tf_op jit(solution)/shard_map/ppermute | solution.py:226
  54.9 2.0 %collective-permute-start.25 = (bf16[4,8,2048]{2,1,0:T(8,128)(2,1)S(1)}, bf16[4,8,2048]{2,1,0:T(8,128)(2,1)S(1)}, u32[]{:S(2)}, u32[]{:S(2)}) collective-permute-start(bf16[4,8,2048]{2,1,0:T(8,128)(2,1)S(1)} %collective-permute-done.21.refs_3_), channel_id=1, source_target_pairs={{0,1},{1,0},{2,3},{3,2},{4,5},{5,4},{6,7},{7,6},{8,9},{9,8},{10,11... | collective-permute-start | bytes 393224 | tf_op jit(solution)/shard_map/ppermute | solution.py:226
  54.9 3.6 %collective-permute-start.7 = (bf16[4,8,2048]{2,1,0:T(8,128)(2,1)S(1)}, bf16[4,8,2048]{2,1,0:T(8,128)(2,1)S(1)}, u32[]{:S(2)}, u32[]{:S(2)}) collective-permute-start(bf16[4,8,2048]{2,1,0:T(8,128)(2,1)S(1)} %finish.2.refs_8_), channel_id=1, source_target_pairs={{0,1},{1,0},{2,3},{3,2},{4,5},{5,4},{6,7},{7,6},{8,9},{9,8},{10,11... | collective-permute-start | bytes 393224 | tf_op jit(solution)/shard_map/ppermute | solution.py:226
  56.3 2.2 %collective-permute-start.11 = (bf16[4,8,2048]{2,1,0:T(8,128)(2,1)S(1)}, bf16[4,8,2048]{2,1,0:T(8,128)(2,1)S(1)}, u32[]{:S(2)}, u32[]{:S(2)}) collective-permute-start(bf16[4,8,2048]{2,1,0:T(8,128)(2,1)S(1)} %collective-permute-done.10.refs_9_), channel_id=1, source_target_pairs={{0,1},{1,0},{2,3},{3,2},{4,5},{5,4},{6,7},{7,6},{8,9},{9,8},{10,11... | collective-permute-start | bytes 393224 | tf_op jit(solution)/shard_map/ppermute | solution.py:226
  56.3 2.2 %collective-permute-start.9 = (bf16[4,8,2048]{2,1,0:T(8,128)(2,1)S(1)}, bf16[4,8,2048]{2,1,0:T(8,128)(2,1)S(1)}, u32[]{:S(2)}, u32[]{:S(2)}) collective-permute-start(bf16[4,8,2048]{2,1,0:T(8,128)(2,1)S(1)} %collective-permute-done.8.refs_10_), channel_id=1, source_target_pairs={{0,1},{1,0},{2,3},{3,2},{4,5},{5,4},{6,7},{7,6},{8,9},{9,8},{10,11... | collective-permute-start | bytes 393224 | tf_op jit(solution)/shard_map/ppermute | solution.py:226
  56.8 1.7 %collective-permute-start.13 = (bf16[4,8,2048]{2,1,0:T(8,128)(2,1)S(1)}, bf16[4,8,2048]{2,1,0:T(8,128)(2,1)S(1)}, u32[]{:S(2)}, u32[]{:S(2)}) collective-permute-start(bf16[4,8,2048]{2,1,0:T(8,128)(2,1)S(1)} %collective-permute-done.12.refs_11_), channel_id=1, source_target_pairs={{0,1},{1,0},{2,3},{3,2},{4,5},{5,4},{6,7},{7,6},{8,9},{9,8},{10,11... | collective-permute-start | bytes 393224 | tf_op jit(solution)/shard_map/ppermute | solution.py:226
